TPU v7x, 32 devices: a whole 2x2x4 slice. The times are simulated.
32 devices in a mesh: azim: 8 (over z, y), row: 4 (over x, core).
Axes of the slice: x: 2, y: 2, z: 4, core: 2. Of those that a mesh axis runs over, the one named last changes fastest.
Arguments:
- flow_state: float32 [6, 4, 16, 1024], P(None, None, 'row', 'azim'), may hold values from -6 to 6
- old_state: float32 [6, 4, 16, 1024], P(None, None, 'row', 'azim'), may hold values from -6 to 6
- local_step: float32 [4, 16, 1024], P(None, 'row', 'azim'), may hold values from 0.2 to 2
- azim_flux: float32 [6, 6], replicated, may hold values from -2.5 to 2.5
- axial_flux: float32 [6, 6], replicated, may hold values from -2.5 to 2.5
- block_inverse: float32 [6, 6, 4, 16, 1024], P(None, None, None, 'row', 'azim'), may hold values from -1 to 1
- lower_block: float32 [6, 6, 4, 16, 1024], P(None, None, None, 'row', 'azim')
- intersection_first: int32 [4, 1024], P('row', 'azim'), may hold values from 0 to 1023, as said below
- intersection_weight: int32 [4, 1024], P('row', 'azim'), may hold values from 0 to 7
Outputs:
- new_state: float32 [6, 4, 16, 1024], P(None, None, 'row', 'azim')
Inputs may be any that keep to these rules, and one draw needn't show every extreme that they name: In each row r, intersection_first[r, a] = (a + o_r) mod 1024 for one offset o_r of that row.
All inputs are finite; a program needn't handle non-finite values.
Results may differ from a plain program's by a relative error of at most 0.0003.
Values sent between devices are 32-bit elements; how exact they have to be, the bound alone decides.
No kernel may reach another device: no remote copies, remote signals or barrier semaphores. Data moves between devices by JAX's collectives and lax.ppermute only.
A program may use at most 128 MiB of HBM per device.

v0:
```python
import functools

import jax
import jax.numpy as jnp
from jax import lax
from jax.experimental import pallas as pl
from jax.experimental.pallas import tpu as pltpu
from jax.sharding import PartitionSpec as P

FIELDS = 6
LANES = 128
HALF = 8
HALO = 72
JST_SECOND = 0.5
JST_FOURTH = 1.0 / 32.0
TIME_FACTOR = 1.5
VMEM = pl.BlockSpec(memory_space=pltpu.VMEM)
HBM = pl.BlockSpec(memory_space=pltpu.HBM)


def lane_ids():
    return lax.broadcasted_iota(jnp.int32, (HALF, LANES), 1)


def roll_lanes(x, shift):
    shift = shift % LANES
    return x if isinstance(shift, int) and shift == 0 else pltpu.roll(x, shift, 1)


def rows(half):
    return pl.ds(half * HALF, HALF)


def packing(sectors):
    return LANES // (2 * sectors)


def product(left, right):
    out = []
    for f in range(FIELDS):
        for h in range(FIELDS):
            acc = left[f * FIELDS] * right[h]
            for g in range(1, FIELDS):
                acc = acc + left[f * FIELDS + g] * right[g * FIELDS + h]
            out.append(acc)
    return out


def matvec(matrix, vector):
    out = []
    for f in range(FIELDS):
        acc = matrix[f * FIELDS] * vector[0]
        for g in range(1, FIELDS):
            acc = acc + matrix[f * FIELDS + g] * vector[g]
        out.append(acc)
    return out


def pack_last_lane(values, lane, base, width):
    acc = jnp.zeros((HALF, LANES), jnp.float32)
    for entry, pair in enumerate(values):
        for half in range(2):
            target = base + width * entry + half
            acc = jnp.where(lane == target, roll_lanes(pair[half], target + 1), acc)
    return acc


def routes(sectors, place, cell):
    turn = (cell // LANES - place) & (sectors - 1)
    flags = []
    for bit in reversed(range(sectors.bit_length() - 1)):
        low = place & ((1 << bit) - 1)
        for k in (turn, (turn + 1) & (sectors - 1)):
            borrow = jnp.where(low < (k & ((1 << bit) - 1)), 1, 0)
            flags.append(((k >> bit) & 1) ^ borrow)
    return flags


def prepare_kernel(
    sectors,
    levels,
    flow_in,
    old_in,
    step_in,
    azf_in,
    axf_in,
    inverse_in,
    lower_in,
    first_in,
    weight_in,
    flow,
    gain,
    source,
    coef,
    flags,
    packed,
    scan,
    old,
    step_size,
    azf,
    axf,
    inverse,
    lower,
    first,
    weight,
    sems,
):
    copies = [
        pltpu.make_async_copy(src, dst, sems.at[at])
        for at, (src, dst) in enumerate(
            (
                (inverse_in, inverse),
                (lower_in, lower),
                (flow_in, flow),
                (old_in, old),
                (step_in, step_size),
                (azf_in, azf),
                (axf_in, axf),
                (first_in, first),
                (weight_in, weight),
            )
        )
    ]
    for copy in copies:
        copy.start()
    lane = lane_ids()
    place = lax.axis_index("azim")
    for copy in copies:
        copy.wait()
    row = lax.broadcasted_iota(jnp.int32, (1, LANES), 1) * 0
    cell = row + jnp.broadcast_to(first[:, 0:1], (1, LANES))
    for at, flag in enumerate(routes(sectors, row + place, cell)):
        flags[pl.ds(at, 1), :] = flag
    flags[pl.ds(flags.shape[0] - 1, 1), :] = cell & (LANES - 1)
    for f in range(FIELDS):
        for g in range(FIELDS):
            at = f * FIELDS + g
            coef[pl.ds(at, 1), :] = jnp.broadcast_to(azf[f : f + 1, g : g + 1], (1, LANES))
            coef[pl.ds(36 + at, 1), :] = jnp.broadcast_to(axf[f : f + 1, g : g + 1], (1, LANES))
    coef[pl.ds(72, 1), :] = (weight[...].astype(jnp.float32) + 0.5) / 8.0
    for half in range(2):
        left = [inverse[e, rows(half), :] for e in range(36)]
        right = [lower[e, rows(half), :] for e in range(36)]
        for e, value in enumerate(product(left, right)):
            scan[e, rows(half), :] = value
    for half in range(2):
        minus_step = -step_size[rows(half), :]
        scaled = [minus_step * inverse[e, rows(half), :] for e in range(36)]
        change = [TIME_FACTOR * (flow[f, rows(half), :] - old[f, rows(half), :]) for f in range(FIELDS)]
        for e in range(36):
            gain[e, rows(half), :] = scaled[e]
        for f, value in enumerate(matvec(scaled, change)):
            source[f, rows(half), :] = value
    for level in range(levels):
        step = 1 << level
        keep = lane < step
        for half in range(2):
            later = [scan[36 * level + e, rows(half), :] for e in range(36)]
            earlier = [roll_lanes(x, step) for x in later]
            for e, value in enumerate(product(later, earlier)):
                scan[36 * (level + 1) + e, rows(half), :] = jnp.where(keep, later[e], value)
    acc = pack_last_lane(
        [[scan[36 * levels + e, rows(half), :] for half in range(2)] for e in range(36)], lane, 0, 2
    )
    for f in range(FIELDS):
        for half in range(2):
            start = HALO + 4 * (2 * f + half)
            u = flow[f, rows(half), :]
            acc = jnp.where((lane >= start) & (lane < start + 2), roll_lanes(u, start), acc)
            acc = jnp.where((lane >= start + 2) & (lane < start + 4), roll_lanes(u, start + 4), acc)
    packed[...] = acc


def jst_parts(u0, um1, um2, up1, up2):
    p0, pm1, pm2, pp1, pp2 = [1.0 + x[0] * x[0] for x in (u0, um1, um2, up1, up2)]

    def sensor(up, mid, down):
        return jnp.abs(up - 2.0 * mid + down) / (up + 2.0 * mid + down)

    mid = sensor(pp1, p0, pm1)
    e2r = JST_SECOND * jnp.maximum(mid, sensor(pp2, pp1, p0))
    e2l = JST_SECOND * jnp.maximum(sensor(p0, pm1, pm2), mid)
    e4r = jnp.maximum(0.0, JST_FOURTH - e2r)
    e4l = jnp.maximum(0.0, JST_FOURTH - e2l)
    central, faces = [], []
    for f in range(FIELDS):
        dr = up1[f] - u0[f]
        dl = u0[f] - um1[f]
        third_r = up2[f] - 3.0 * up1[f] + 3.0 * u0[f] - um1[f]
        third_l = up1[f] - 3.0 * u0[f] + 3.0 * um1[f] - um2[f]
        central.append(0.5 * (up1[f] - um1[f]))
        faces.append((e2r * dr - e4r * third_r) - (e2l * dl - e4l * third_l))
    return central, faces


def position(sectors, difference):
    bits = sectors.bit_length() - 1
    at = 0
    for bit in range(bits):
        at = at + (((difference >> bit) & 1) << (bits - 1 - bit))
    return at


def source_kernel(
    sectors, levels, ring_a, ring_b, ring, flow, gain, source, coef, flags, scan, sweep, packed
):
    lane = lane_ids()
    sub = lax.broadcasted_iota(jnp.int32, (HALF, LANES), 0)
    place = lax.axis_index("azim")
    row = lax.axis_index("row")
    left_pack = ring[position(sectors, place ^ ((place + sectors - 1) & (sectors - 1)))]
    right_pack = ring[position(sectors, place ^ ((place + 1) & (sectors - 1)))]
    shift = flags[flags.shape[0] - 1, 0]
    back = (LANES - shift) & (LANES - 1)

    def coefficient(at):
        return jnp.broadcast_to(coef[pl.ds(at, 1), :], (HALF, LANES))

    frac = coefficient(72)
    ghost = []
    for f in range(FIELDS):
        a = pltpu.roll(ring_a[pl.ds(f * HALF, HALF), :], back, 1)
        b = pltpu.roll(ring_b[pl.ds(f * HALF, HALF), :], back, 1)
        one = jnp.where(lane < LANES - shift, a, b)
        two = pltpu.roll(jnp.where(lane == 0, b, one), LANES - 1, 1)
        ghost.append(frac * one + (1.0 - frac) * two)
    halo = jnp.where((lane & 3) < 2, right_pack, left_pack)
    axial = sub % 4
    is_first_row = row == 0
    for half in range(2):
        u0 = [flow[f, rows(half), :] for f in range(FIELDS)]
        um1, um2, up1, up2 = [], [], [], []
        for f in range(FIELDS):
            start = HALO + 4 * (2 * f + half)
            edge = roll_lanes(halo, LANES - 2 - start)
            um1.append(jnp.where(lane < 1, roll_lanes(halo, -(start + 3)), roll_lanes(u0[f], 1)))
            um2.append(jnp.where(lane < 2, edge, roll_lanes(u0[f], 2)))
            up1.append(jnp.where(lane >= LANES - 1, roll_lanes(halo, LANES - 1 - start), roll_lanes(u0[f], -1)))
            up2.append(jnp.where(lane >= LANES - 2, edge, roll_lanes(u0[f], -2)))
        az_central, az_faces = jst_parts(u0, um1, um2, up1, up2)
        um1, um2, up1, up2 = [], [], [], []
        for f in range(FIELDS):
            g = ghost[f]
            if half == 0:
                spread = jnp.where(sub < 4, g, pltpu.roll(g, 2, 0))
            else:
                spread = jnp.where(sub < 4, pltpu.roll(g, 4, 0), pltpu.roll(g, 6, 0))
            u = u0[f]
            down1 = pltpu.roll(u, 1, 0)
            down2 = pltpu.roll(u, 2, 0)
            lift1 = pltpu.roll(u, HALF - 1, 0)
            lift2 = pltpu.roll(u, HALF - 2, 0)
            same = jnp.where(axial == 0, u, down1)
            spread = jnp.where(is_first_row, same, spread)
            next_ghost = pltpu.roll(spread, HALF - 1, 0)
            um1.append(jnp.where(axial == 0, next_ghost, down1))
            um2.append(jnp.where(axial < 2, spread, down2))
            last1 = jnp.where(axial == 3, u, lift1)
            up1.append(last1)
            up2.append(jnp.where(axial == 3, u, jnp.where(axial == 2, lift1, lift2)))
        ax_central, ax_faces = jst_parts(u0, um1, um2, up1, up2)
        residual = []
        for f in range(FIELDS):
            acc = -(az_faces[f] + ax_faces[f])
            for g in range(FIELDS):
                at = f * FIELDS + g
                acc = acc + coefficient(at) * az_central[g] + coefficient(36 + at) * ax_central[g]
            residual.append(acc)
        added = matvec([gain[e, rows(half), :] for e in range(36)], residual)
        for f in range(FIELDS):
            sweep[f, rows(half), :] = source[f, rows(half), :] + added[f]
    values = [[sweep[f, rows(half), :] for half in range(2)] for f in range(FIELDS)]
    for level in range(levels):
        step = 1 << level
        for half in range(2):
            before = [jnp.where(lane < step, 0.0, roll_lanes(values[f][half], step)) for f in range(FIELDS)]
            matrix = [scan[36 * level + e, rows(half), :] for e in range(36)]
            for f, gain in enumerate(matvec(matrix, before)):
                values[f][half] = values[f][half] + gain
    for f in range(FIELDS):
        for half in range(2):
            sweep[f, rows(half), :] = values[f][half]
    per = packing(sectors)
    for at in range(0, FIELDS, per):
        value = pack_last_lane(values[at : at + per], lane, 0, 2 * sectors)
        packed[pl.ds(HALF * (at // per), HALF), :] = roll_lanes(value, 2 * place)


def relative(pack, entry, sectors, place, lane):
    per = packing(sectors)
    width = 2 * sectors
    base = (entry % per) * width
    row = pack[pl.ds(HALF * (entry // per), HALF), :]
    turn = 2 * place
    here = pltpu.roll(row, lax.rem(2 * LANES - base - turn, LANES), 1)
    wrapped = pltpu.roll(row, lax.rem(2 * LANES - base - turn + width, LANES), 1)
    return jnp.where(lane < width - turn, here, wrapped)


def closing_kernel(sectors, ring, suffix, closing):
    lane = lane_ids()
    place = lax.axis_index("azim")
    width = 2 * sectors
    one = [jnp.float32(1.0 if e % 7 == 0 else 0.0) for e in range(36)]
    turned = []
    for t in range(sectors):
        at = position(sectors, place ^ ((place + t) & (sectors - 1)))
        turned.append(roll_lanes(ring[at], 2 * t))
    pair = lane >> 1
    maps = []
    for e in range(36):
        acc = turned[0]
        for t in range(1, sectors):
            acc = jnp.where(pair == (e + t) % (LANES // 2), turned[t], acc)
        maps.append(roll_lanes(acc, -2 * e))
    step = 2
    while step < width:
        later = [jnp.where(lane < width - step, roll_lanes(x, -step), one[e]) for e, x in enumerate(maps)]
        maps = product(later, maps)
        step *= 2
    for e in range(36):
        suffix[e] = jnp.where(lane < width - 2, roll_lanes(maps[e], -2), one[e])
    system = [[one[f * 6 + g] - maps[f * 6 + g] for g in range(6)] for f in range(6)]
    result = [[jnp.full((HALF, LANES), one[f * 6 + g]) for g in range(6)] for f in range(6)]
    for pivot in range(6):
        scale = 1.0 / system[pivot][pivot]
        for g in range(pivot + 1, 6):
            system[pivot][g] = system[pivot][g] * scale
        for g in range(pivot + 1):
            result[pivot][g] = result[pivot][g] * scale
        for f in range(6):
            if f == pivot:
                continue
            factor = system[f][pivot]
            for g in range(pivot + 1, 6):
                system[f][g] = system[f][g] - factor * system[pivot][g]
            for g in range(pivot + 1):
                result[f][g] = result[f][g] - factor * result[pivot][g]
    for f in range(6):
        for g in range(6):
            closing[f * 6 + g] = result[f][g]


def finish_kernel(sectors, levels, gathered, suffix, closing, flow, scan, sweep, out):
    lane = lane_ids()
    place = lax.axis_index("azim")
    width = 2 * sectors
    ends = [relative(gathered, f, sectors, place, lane) for f in range(FIELDS)]
    total = matvec([suffix[e] for e in range(36)], ends)
    step = width // 2
    while step >= 2:
        total = [x + roll_lanes(x, -step) for x in total]
        step //= 2
    start = matvec([closing[e] for e in range(36)], total)
    for half in range(2):
        begin = [jnp.broadcast_to(x[:, half : half + 1], (HALF, LANES)) for x in start]
        gain = matvec([scan[e, rows(half), :] for e in range(36)], begin)
        for f in range(FIELDS):
            out[f, rows(half), :] = flow[f, rows(half), :] + (gain[f] + sweep[f, rows(half), :])


def shape(*dims):
    return jax.ShapeDtypeStruct(dims, jnp.float32)


def shards(
    sectors,
    row_count,
    flow_state,
    old_state,
    local_step,
    azim_flux,
    axial_flux,
    block_inverse,
    lower_block,
    intersection_first,
    intersection_weight,
):
    radial, axial, cells = flow_state.shape[1:]
    lines = radial * axial
    levels = cells.bit_length() - 1
    end_rows = HALF * pl.cdiv(FIELDS, packing(sectors))
    flag_rows = HALF * pl.cdiv(2 * sectors.bit_length() - 1, HALF)
    call = functools.partial(
        pl.pallas_call, compiler_params=pltpu.CompilerParams(vmem_limit_bytes=16 << 20)
    )

    upstream = lax.ppermute(flow_state, "row", [(r, (r + 1) % row_count) for r in range(row_count)])
    flow, gain, source, coef, flags, ring, scan = call(
        functools.partial(prepare_kernel, sectors, levels),
        out_shape=(
            shape(FIELDS, lines, cells),
            shape(36, lines, cells),
            shape(FIELDS, lines, cells),
            shape(80, cells),
            jax.ShapeDtypeStruct((flag_rows, cells), jnp.int32),
            shape(HALF, cells),
            shape(36 * (levels + 1), lines, cells),
        ),
        in_specs=[HBM] * 9,
        out_specs=(VMEM,) * 7,
        scratch_shapes=[
            pltpu.VMEM((FIELDS, lines, cells), jnp.float32),
            pltpu.VMEM((lines, cells), jnp.float32),
            pltpu.VMEM((FIELDS, FIELDS), jnp.float32),
            pltpu.VMEM((FIELDS, FIELDS), jnp.float32),
            pltpu.VMEM((36, lines, cells), jnp.float32),
            pltpu.VMEM((36, lines, cells), jnp.float32),
            pltpu.VMEM((1, cells), jnp.int32),
            pltpu.VMEM((1, cells), jnp.int32),
            pltpu.SemaphoreType.DMA((9,)),
        ],
    )(
        *(
            pltpu.with_memory_space_constraint(x, pltpu.HBM)
            for x in (
                flow_state.reshape(FIELDS, lines, cells),
                old_state.reshape(FIELDS, lines, cells),
                local_step.reshape(lines, cells),
                azim_flux,
                axial_flux,
                block_inverse.reshape(36, lines, cells),
                lower_block.reshape(36, lines, cells),
                intersection_first,
                intersection_weight,
            )
        )
    )
    ring_a = ring_b = upstream[:, :, axial - 2 :, :].reshape(FIELDS * HALF, cells)
    at, mask = 0, sectors // 2
    while mask:
        from_a = flags[at : at + 1] != 0
        from_b = flags[at + 1 : at + 2] != 0
        sent = jnp.concatenate([jnp.where(from_a, ring_a, ring_b), ring], axis=0)
        arrived = lax.ppermute(sent, "azim", [(i, i ^ mask) for i in range(sectors)])
        upper = arrived[: FIELDS * HALF]
        ring_a = jnp.where(from_a, upper, ring_a)
        ring_b = jnp.where(from_b, upper, ring_b)
        ring = jnp.concatenate([ring, arrived[FIELDS * HALF :]], axis=0)
        at, mask = at + 2, mask // 2
    ring = ring.reshape(sectors, HALF, cells)

    sweep, ends = call(
        functools.partial(source_kernel, sectors, levels),
        out_shape=(shape(FIELDS, lines, cells), shape(end_rows, cells)),
        in_specs=[VMEM] * 9,
        out_specs=(VMEM, VMEM),
    )(ring_a, ring_b, ring, flow, gain, source, coef, flags, scan)
    suffix, closing = call(
        functools.partial(closing_kernel, sectors),
        out_shape=(shape(36, HALF, LANES), shape(36, HALF, LANES)),
        in_specs=[VMEM],
        out_specs=(VMEM, VMEM),
    )(ring)
    mask = 1
    while mask < sectors:
        ends = ends + lax.ppermute(ends, "azim", [(i, i ^ mask) for i in range(sectors)])
        mask *= 2
    new_state = call(
        functools.partial(finish_kernel, sectors, levels),
        out_shape=shape(FIELDS, lines, cells),
        in_specs=[VMEM] * 6,
        out_specs=VMEM,
    )(ends, suffix, closing, flow, scan[36 * levels :], sweep)
    return new_state.reshape(flow_state.shape)


def solution(mesh):
    return jax.shard_map(
        functools.partial(shards, mesh.shape["azim"], mesh.shape["row"]),
        mesh=mesh,
        in_specs=(
            P(None, None, "row", "azim"),
            P(None, None, "row", "azim"),
            P(None, "row", "azim"),
            P(),
            P(),
            P(None, None, None, "row", "azim"),
            P(None, None, None, "row", "azim"),
            P("row", "azim"),
            P("row", "azim"),
        ),
        out_specs=P(None, None, "row", "azim"),
        check_vma=False,
    )
```

profile of v0, /device:TPU:0, one launch (start us, length us, event | category | flops | bytes accessed | tf_op | source)
XLA Modules:
  0.0 31.7 jit_solution(3756097252220959236)
XLA Ops:
  0.0 0.5 %collective-permute-start = (f32[6,4,4,128]{3,2,1,0:T(4,128)}, f32[6,4,4,128]{3,2,1,0:T(4,128)S(1)}, u32[]{:S(2)}, u32[]{:S(2)}) collective-permute-start(f32[6,4,4,128]{3,2,1,0:T(4,128)} %param.9), channel_id=1, source_target_pairs={{0,1},{1,2},{2,3},{3,0},{4,5},{5,6},{6,7},{7,4},{8,9},{9,10},{10,1... | collective-permute-start | bytes 147464 | tf_op jit(solution)/shard_map/ppermute | solution.py:388
  0.5 2.4 %shard_map.91 = (f32[6,16,128]{2,1,0:T(8,128)S(1)}, f32[36,16,128]{2,1,0:T(8,128)S(1)}, f32[6,16,128]{2,1,0:T(8,128)S(1)}, f32[80,128]{1,0:T(8,128)S(1)}, s32[8,...) custom-call(f32[6,16,128]{2,1,0:T(8,128)} %bitcast.27, f32[6,16,128]{2,1,0:T(8,128)} %bitcast.26, ...), custom_call_target="tpu_custom_call" | custom-call | tf_op jit(solution)/shard_map/pallas_call | solution.py:389
  2.9 1.5 %collective-permute-done = f32[6,4,4,128]{3,2,1,0:T(4,128)S(1)} collective-permute-done((f32[6,4,4,128]{3,2,1,0:T(4,128)}, f32[6,4,4,128]{3,2,1,0:T(4,128)S(1)}, u32[]{:S(2)}, u32[]{:S(2)}) %collective-permute-start) | collective-permute-done | bytes 49184 | tf_op jit(solution)/shard_map/ppermute | solution.py:388
  4.4 3.5 %collective-permute-start.1 = (f32[56,128]{1,0:T(8,128)S(1)}, f32[56,128]{1,0:T(8,128)S(1)}, u32[]{:S(2)}, u32[]{:S(2)}) collective-permute-start(f32[56,128]{1,0:T(8,128)S(1)} %pad_maximum_fusion.2), channel_id=1, source_target_pairs={{0,16},{4,20},{8,24},{12,28},{16,0},{20,4},{24,8},{28,12},{1,17},{... | collective-permute-start | bytes 86024 | tf_op jit(solution)/shard_map/ppermute | solution.py:435
  7.9 1.8 %collective-permute-done.1 = f32[56,128]{1,0:T(8,128)S(1)} collective-permute-done((f32[56,128]{1,0:T(8,128)S(1)}, f32[56,128]{1,0:T(8,128)S(1)}, u32[]{:S(2)}, u32[]{:S(2)}) %collective-permute-start.1) | collective-permute-done | bytes 28704 | tf_op jit(solution)/shard_map/ppermute | solution.py:435
  9.8 2.0 %collective-permute-start.2 = (f32[64,128]{1,0:T(8,128)S(1)}, f32[64,128]{1,0:T(8,128)S(1)}, u32[]{:S(2)}, u32[]{:S(2)}) collective-permute-start(f32[64,128]{1,0:T(8,128)S(1)} %pad_maximum_fusion.1), channel_id=1, source_target_pairs={{0,8},{4,12},{8,0},{12,4},{16,24},{20,28},{24,16},{28,20},{1,9},{5... | collective-permute-start | bytes 98312 | tf_op jit(solution)/shard_map/ppermute | solution.py:435
  11.7 2.0 %collective-permute-done.2 = f32[64,128]{1,0:T(8,128)S(1)} collective-permute-done((f32[64,128]{1,0:T(8,128)S(1)}, f32[64,128]{1,0:T(8,128)S(1)}, u32[]{:S(2)}, u32[]{:S(2)}) %collective-permute-start.2) | collective-permute-done | bytes 32800 | tf_op jit(solution)/shard_map/ppermute | solution.py:435
  13.8 1.9 %collective-permute-start.3 = (f32[80,128]{1,0:T(8,128)S(1)}, f32[80,128]{1,0:T(8,128)S(1)}, u32[]{:S(2)}, u32[]{:S(2)}) collective-permute-start(f32[80,128]{1,0:T(8,128)S(1)} %pad_maximum_fusion), channel_id=1, source_target_pairs={{0,4},{4,0},{8,12},{12,8},{16,20},{20,16},{24,28},{28,24},{1,5},{5... | collective-permute-start | bytes 122888 | tf_op jit(solution)/shard_map/ppermute | solution.py:435
  15.7 2.2 %collective-permute-done.3 = f32[80,128]{1,0:T(8,128)S(1)} collective-permute-done((f32[80,128]{1,0:T(8,128)S(1)}, f32[80,128]{1,0:T(8,128)S(1)}, u32[]{:S(2)}, u32[]{:S(2)}) %collective-permute-start.3) | collective-permute-done | bytes 40992 | tf_op jit(solution)/shard_map/ppermute | solution.py:435
  17.9 1.0 %shard_map.92 = (f32[6,16,128]{2,1,0:T(8,128)S(1)}, f32[8,128]{1,0:T(8,128)S(1)}) custom-call(f32[48,128]{1,0:T(8,128)S(1)} %get-tuple-element.31.ring_a, f32[48,128]{1,0:T(8,128)S(1)} %get-tuple-element.30.ring_b, f32[8,8,128]{2,1,0:T(8,128)S(1)} %maximum_bitcast_fusion.ring, f32[6,16,128]{2,1,0:T(8,128)S(1)} %get-tuple-element.18.flow, ...), custom_call_target="tpu_custom_call" | custom-call | tf_op jit(solution)/shard_map/pallas_call | solution.py:443
  18.9 1.9 %collective-permute-start.4 = (f32[8,128]{1,0:T(8,128)S(1)}, f32[8,128]{1,0:T(8,128)S(1)}, u32[]{:S(2)}, u32[]{:S(2)}) collective-permute-start(f32[8,128]{1,0:T(8,128)S(1)} %get-tuple-element.23), channel_id=1, source_target_pairs={{0,4},{4,0},{8,12},{12,8},{16,20},{20,16},{24,28},{28,24},{1,5},{5... | collective-permute-start | bytes 12296 | tf_op jit(solution)/shard_map/ppermute | solution.py:457
  20.8 1.8 %collective-permute-done.4 = f32[8,128]{1,0:T(8,128)S(1)} collective-permute-done((f32[8,128]{1,0:T(8,128)S(1)}, f32[8,128]{1,0:T(8,128)S(1)}, u32[]{:S(2)}, u32[]{:S(2)}) %collective-permute-start.4) | collective-permute-done | bytes 4128 | tf_op jit(solution)/shard_map/ppermute | solution.py:457
  22.5 1.9 %collective-permute-start.5 = (f32[8,128]{1,0:T(8,128)S(1)}, f32[8,128]{1,0:T(8,128)S(1)}, u32[]{:S(2)}, u32[]{:S(2)}) collective-permute-start(f32[8,128]{1,0:T(8,128)S(1)} %add.9), channel_id=1, source_target_pairs={{0,8},{4,12},{8,0},{12,4},{16,24},{20,28},{24,16},{28,20},{1,9},{5... | collective-permute-start | bytes 12296 | tf_op jit(solution)/shard_map/ppermute | solution.py:457
  24.4 1.7 %collective-permute-done.5 = f32[8,128]{1,0:T(8,128)S(1)} collective-permute-done((f32[8,128]{1,0:T(8,128)S(1)}, f32[8,128]{1,0:T(8,128)S(1)}, u32[]{:S(2)}, u32[]{:S(2)}) %collective-permute-start.5) | collective-permute-done | bytes 4128 | tf_op jit(solution)/shard_map/ppermute | solution.py:457
  26.1 2.9 %collective-permute-start.6 = (f32[8,128]{1,0:T(8,128)S(1)}, f32[8,128]{1,0:T(8,128)S(1)}, u32[]{:S(2)}, u32[]{:S(2)}) collective-permute-start(f32[8,128]{1,0:T(8,128)S(1)} %add.10), channel_id=1, source_target_pairs={{0,16},{4,20},{8,24},{12,28},{16,0},{20,4},{24,8},{28,12},{1,17},{... | collective-permute-start | bytes 12296 | tf_op jit(solution)/shard_map/ppermute | solution.py:457
  29.1 0.6 %shard_map.93 = (f32[36,8,128]{2,1,0:T(8,128)S(1)}, f32[36,8,128]{2,1,0:T(8,128)S(1)}) custom-call(f32[8,8,128]{2,1,0:T(8,128)S(1)} %maximum_bitcast_fusion.ring), custom_call_target="tpu_custom_call" | custom-call | tf_op jit(solution)/shard_map/pallas_call | solution.py:449
  29.6 1.0 %collective-permute-done.6 = f32[8,128]{1,0:T(8,128)S(1)} collective-permute-done((f32[8,128]{1,0:T(8,128)S(1)}, f32[8,128]{1,0:T(8,128)S(1)}, u32[]{:S(2)}, u32[]{:S(2)}) %collective-permute-start.6) | collective-permute-done | bytes 4128 | tf_op jit(solution)/shard_map/ppermute | solution.py:457
  30.6 1.0 %shard_map.94 = f32[6,16,128]{2,1,0:T(8,128)} custom-call(f32[8,128]{1,0:T(8,128)S(1)} %add.11.gathered, f32[36,8,128]{2,1,0:T(8,128)S(1)} %get-tuple-element.24.suffix, f32[36,8,128]{2,1,0:T(8,128)S(1)} %get-tuple-element.25.closing, f32[6,16,128]{2,1,0:T(8,128)S(1)} %get-tuple-element.18.flow, f32[36,16,128]{2,1,0:T(8,128)S(1)} %slice.55.scan, ...), custom_call_target="tpu_custom_call" | custom-call | tf_op jit(solution)/shard_map/pallas_call | solution.py:459
  (16 shorter events, 0.1 us)
Async XLA Ops:
  0.0 4.4 %collective-permute-start = (f32[6,4,4,128]{3,2,1,0:T(4,128)}, f32[6,4,4,128]{3,2,1,0:T(4,128)S(1)}, u32[]{:S(2)}, u32[]{:S(2)}) collective-permute-start(f32[6,4,4,128]{3,2,1,0:T(4,128)} %param.9), channel_id=1, source_target_pairs={{0,1},{1,2},{2,3},{3,0},{4,5},{5,6},{6,7},{7,4},{8,9},{9,10},{10,1... | collective-permute-start | bytes 147464 | tf_op jit(solution)/shard_map/ppermute | solution.py:388
  4.4 5.3 %collective-permute-start.1 = (f32[56,128]{1,0:T(8,128)S(1)}, f32[56,128]{1,0:T(8,128)S(1)}, u32[]{:S(2)}, u32[]{:S(2)}) collective-permute-start(f32[56,128]{1,0:T(8,128)S(1)} %pad_maximum_fusion.2), channel_id=1, source_target_pairs={{0,16},{4,20},{8,24},{12,28},{16,0},{20,4},{24,8},{28,12},{1,17},{... | collective-permute-start | bytes 86024 | tf_op jit(solution)/shard_map/ppermute | solution.py:435
  9.8 4.0 %collective-permute-start.2 = (f32[64,128]{1,0:T(8,128)S(1)}, f32[64,128]{1,0:T(8,128)S(1)}, u32[]{:S(2)}, u32[]{:S(2)}) collective-permute-start(f32[64,128]{1,0:T(8,128)S(1)} %pad_maximum_fusion.1), channel_id=1, source_target_pairs={{0,8},{4,12},{8,0},{12,4},{16,24},{20,28},{24,16},{28,20},{1,9},{5... | collective-permute-start | bytes 98312 | tf_op jit(solution)/shard_map/ppermute | solution.py:435
  13.8 4.1 %collective-permute-start.3 = (f32[80,128]{1,0:T(8,128)S(1)}, f32[80,128]{1,0:T(8,128)S(1)}, u32[]{:S(2)}, u32[]{:S(2)}) collective-permute-start(f32[80,128]{1,0:T(8,128)S(1)} %pad_maximum_fusion), channel_id=1, source_target_pairs={{0,4},{4,0},{8,12},{12,8},{16,20},{20,16},{24,28},{28,24},{1,5},{5... | collective-permute-start | bytes 122888 | tf_op jit(solution)/shard_map/ppermute | solution.py:435
  18.9 3.6 %collective-permute-start.4 = (f32[8,128]{1,0:T(8,128)S(1)}, f32[8,128]{1,0:T(8,128)S(1)}, u32[]{:S(2)}, u32[]{:S(2)}) collective-permute-start(f32[8,128]{1,0:T(8,128)S(1)} %get-tuple-element.23), channel_id=1, source_target_pairs={{0,4},{4,0},{8,12},{12,8},{16,20},{20,16},{24,28},{28,24},{1,5},{5... | collective-permute-start | bytes 12296 | tf_op jit(solution)/shard_map/ppermute | solution.py:457
  22.5 3.6 %collective-permute-start.5 = (f32[8,128]{1,0:T(8,128)S(1)}, f32[8,128]{1,0:T(8,128)S(1)}, u32[]{:S(2)}, u32[]{:S(2)}) collective-permute-start(f32[8,128]{1,0:T(8,128)S(1)} %add.9), channel_id=1, source_target_pairs={{0,8},{4,12},{8,0},{12,4},{16,24},{20,28},{24,16},{28,20},{1,9},{5... | collective-permute-start | bytes 12296 | tf_op jit(solution)/shard_map/ppermute | solution.py:457
  26.1 4.5 %collective-permute-start.6 = (f32[8,128]{1,0:T(8,128)S(1)}, f32[8,128]{1,0:T(8,128)S(1)}, u32[]{:S(2)}, u32[]{:S(2)}) collective-permute-start(f32[8,128]{1,0:T(8,128)S(1)} %add.10), channel_id=1, source_target_pairs={{0,16},{4,20},{8,24},{12,28},{16,0},{20,4},{24,8},{28,12},{1,17},{... | collective-permute-start | bytes 12296 | tf_op jit(solution)/shard_map/ppermute | solution.py:457
where the time goes:
time: 31.8 us; the launch traced here: 31.7 us
  starting transfers between devices  14.5 us (46%)
  waiting for transfers between devices  11.9 us (37%)
  Pallas kernels  5.03 us (16%)
    ppermute x3, starting transfers between devices, shards(): lax.ppermute(sent, 'azim', [(i, i ^ mask) for i in range(sectors)])  7.35 us
    ppermute x3, starting transfers between devices, shards(): lax.ppermute(ends, 'azim', [(i, i ^ mask) for i in range(sectors)])  6.68 us
    ppermute x3, waiting for transfers between devices, shards(): lax.ppermute(sent, 'azim', [(i, i ^ mask) for i in range(sectors)])  6 us
    ppermute x3, waiting for transfers between devices, shards(): lax.ppermute(ends, 'azim', [(i, i ^ mask) for i in range(sectors)])  4.46 us
    pallas_call x1, Pallas kernels, shards(): call(functools.partial(prepare_kernel, sectors, levels), out_shape=(shape...  2.42 us
    ppermute x1, waiting for transfers between devices, shards(): lax.ppermute(flow_state, 'row', [(r, (r + 1) % row_count) for r in range(...  1.46 us
    pallas_call x1, Pallas kernels, shards(): call(functools.partial(source_kernel, sectors, levels), out_shape=(shape(...  1.03 us
    pallas_call x1, Pallas kernels, shards(): call(functools.partial(finish_kernel, sectors, levels), out_shape=shape(F...  1.02 us
  transfers between devices with their start and end apart: 7, of which 7 were waited for; matrix products, arithmetic and copies ran while one was open for 0% of the time, Pallas kernels for 9%

commit v1 on v0

--- a/solution.py
+++ b/solution.py
@@ -65,21 +65,54 @@
     return acc
 
 
+def groups(sectors):
+    bits = sectors.bit_length() - 1
+    found = []
+    for low in reversed(range(0, bits - 1, 2)):
+        found.append((1 << low, 2 << low, 3 << low))
+    return found
+
+
 def routes(sectors, place, cell):
     turn = (cell // LANES - place) & (sectors - 1)
+    turns = (turn, (turn + 1) & (sectors - 1))
     flags = []
-    for bit in reversed(range(sectors.bit_length() - 1)):
-        low = place & ((1 << bit) - 1)
-        for k in (turn, (turn + 1) & (sectors - 1)):
-            borrow = jnp.where(low < (k & ((1 << bit) - 1)), 1, 0)
-            flags.append(((k >> bit) & 1) ^ borrow)
+    half = sectors // 2
+    for k in turns:
+        borrow = jnp.where((place & (half - 1)) < (k & (half - 1)), half, 0)
+        flags.append((k & half) ^ borrow)
+    for unit, _, _ in groups(sectors):
+        span = 4 * unit - 1
+        mine = place & span & -unit
+        for k in turns:
+            low = (place - k) & (unit - 1)
+            flags.append(mine ^ ((mine + low + k) & span & -unit))
+        flags.append(mine ^ ((place - turn) & span & -unit))
     return flags
+
+
+def edges_kernel(flow_in, flow, outlet, halo, sem):
+    copy = pltpu.make_async_copy(flow_in, flow, sem)
+    copy.start()
+    lane = lane_ids()
+    sub = lax.broadcasted_iota(jnp.int32, (HALF, LANES), 0)
+    copy.wait()
+    acc = jnp.zeros((HALF, LANES), jnp.float32)
+    for f in range(FIELDS):
+        lower, upper = flow[f, rows(0), :], flow[f, rows(1), :]
+        outlet[pl.ds(f * HALF, HALF), :] = jnp.where((sub & 3) >= 2, lower, pltpu.roll(upper, HALF - 2, 0))
+        for half, u in enumerate((lower, upper)):
+            start = HALO + 4 * (2 * f + half)
+            acc = jnp.where((lane >= start) & (lane < start + 2), roll_lanes(u, start), acc)
+            acc = jnp.where((lane >= start + 2) & (lane < start + 4), roll_lanes(u, start + 4), acc)
+    halo[...] = acc
 
 
 def prepare_kernel(
     sectors,
     levels,
-    flow_in,
+    flow,
+    halo,
     old_in,
     step_in,
     azf_in,
@@ -88,7 +121,6 @@
     lower_in,
     first_in,
     weight_in,
-    flow,
     gain,
     source,
     coef,
@@ -111,7 +143,6 @@
             (
                 (inverse_in, inverse),
                 (lower_in, lower),
-                (flow_in, flow),
                 (old_in, old),
                 (step_in, step_size),
                 (azf_in, azf),
@@ -162,13 +193,7 @@
     acc = pack_last_lane(
         [[scan[36 * levels + e, rows(half), :] for half in range(2)] for e in range(36)], lane, 0, 2
     )
-    for f in range(FIELDS):
-        for half in range(2):
-            start = HALO + 4 * (2 * f + half)
-            u = flow[f, rows(half), :]
-            acc = jnp.where((lane >= start) & (lane < start + 2), roll_lanes(u, start), acc)
-            acc = jnp.where((lane >= start + 2) & (lane < start + 4), roll_lanes(u, start + 4), acc)
-    packed[...] = acc
+    packed[...] = jnp.where(lane < HALO, acc, halo[...])
 
 
 def jst_parts(u0, um1, um2, up1, up2):
@@ -193,12 +218,20 @@
     return central, faces
 
 
-def position(sectors, difference):
-    bits = sectors.bit_length() - 1
-    at = 0
-    for bit in range(bits):
-        at = at + (((difference >> bit) & 1) << (bits - 1 - bit))
+def gathered_at(sectors, difference):
+    at, count = 0, 1
+    for unit, _, _ in groups(sectors):
+        at = at + ((difference // unit) & 3) * count
+        count *= 4
     return at
+
+
+def halo_at(sectors, difference):
+    return 2 * gathered_at(sectors, difference) + difference // (sectors // 2)
+
+
+def map_at(sectors, difference):
+    return gathered_at(sectors, difference) + (difference // (sectors // 2)) * (sectors // 2)
 
 
 def source_kernel(
@@ -208,8 +241,8 @@
     sub = lax.broadcasted_iota(jnp.int32, (HALF, LANES), 0)
     place = lax.axis_index("azim")
     row = lax.axis_index("row")
-    left_pack = ring[position(sectors, place ^ ((place + sectors - 1) & (sectors - 1)))]
-    right_pack = ring[position(sectors, place ^ ((place + 1) & (sectors - 1)))]
+    left_pack = ring[halo_at(sectors, place ^ ((place + sectors - 1) & (sectors - 1)))]
+    right_pack = ring[halo_at(sectors, place ^ ((place + 1) & (sectors - 1)))]
     shift = flags[flags.shape[0] - 1, 0]
     back = (LANES - shift) & (LANES - 1)
 
@@ -241,10 +274,7 @@
         um1, um2, up1, up2 = [], [], [], []
         for f in range(FIELDS):
             g = ghost[f]
-            if half == 0:
-                spread = jnp.where(sub < 4, g, pltpu.roll(g, 2, 0))
-            else:
-                spread = jnp.where(sub < 4, pltpu.roll(g, 4, 0), pltpu.roll(g, 6, 0))
+            spread = pltpu.roll(g, HALF - 2, 0) if half == 0 else g
             u = u0[f]
             down1 = pltpu.roll(u, 1, 0)
             down2 = pltpu.roll(u, 2, 0)
@@ -304,7 +334,7 @@
     one = [jnp.float32(1.0 if e % 7 == 0 else 0.0) for e in range(36)]
     turned = []
     for t in range(sectors):
-        at = position(sectors, place ^ ((place + t) & (sectors - 1)))
+        at = map_at(sectors, place ^ ((place + t) & (sectors - 1)))
         turned.append(roll_lanes(ring[at], 2 * t))
     pair = lane >> 1
     maps = []
@@ -354,9 +384,29 @@
     start = matvec([closing[e] for e in range(36)], total)
     for half in range(2):
         begin = [jnp.broadcast_to(x[:, half : half + 1], (HALF, LANES)) for x in start]
-        gain = matvec([scan[e, rows(half), :] for e in range(36)], begin)
+        gain = matvec([scan[36 * levels + e, rows(half), :] for e in range(36)], begin)
         for f in range(FIELDS):
             out[f, rows(half), :] = flow[f, rows(half), :] + (gain[f] + sweep[f, rows(half), :])
+
+
+def exchange(values, sectors, mask):
+    return lax.ppermute(values, "azim", [(i, i ^ mask) for i in range(sectors)])
+
+
+def from_upstream(values, sectors, row_count, mask):
+    return lax.ppermute(
+        values,
+        ("azim", "row"),
+        [
+            (i * row_count + r, (i ^ mask) * row_count + (r + 1) % row_count)
+            for i in range(sectors)
+            for r in range(row_count)
+        ],
+    )
+
+
+def in_hbm(x):
+    return pltpu.with_memory_space_constraint(x, pltpu.HBM)
 
 
 def shape(*dims):
@@ -380,16 +430,26 @@
     lines = radial * axial
     levels = cells.bit_length() - 1
     end_rows = HALF * pl.cdiv(FIELDS, packing(sectors))
-    flag_rows = HALF * pl.cdiv(2 * sectors.bit_length() - 1, HALF)
+    flag_rows = HALF * pl.cdiv(3 * sectors.bit_length(), HALF)
+    count = FIELDS * HALF
     call = functools.partial(
         pl.pallas_call, compiler_params=pltpu.CompilerParams(vmem_limit_bytes=16 << 20)
     )
 
-    upstream = lax.ppermute(flow_state, "row", [(r, (r + 1) % row_count) for r in range(row_count)])
-    flow, gain, source, coef, flags, ring, scan = call(
+    flow, outlet, halo = call(
+        edges_kernel,
+        out_shape=(shape(FIELDS, lines, cells), shape(count, cells), shape(HALF, cells)),
+        in_specs=[HBM],
+        out_specs=(VMEM,) * 3,
+        scratch_shapes=[pltpu.SemaphoreType.DMA(())],
+    )(in_hbm(flow_state.reshape(FIELDS, lines, cells)))
+    top = sectors // 2
+    upstream_far = from_upstream(outlet, sectors, row_count, top)
+    halo_far = exchange(halo, sectors, top)
+    upstream = from_upstream(outlet, sectors, row_count, 0)
+    gain, source, coef, flags, packed, scan = call(
         functools.partial(prepare_kernel, sectors, levels),
         out_shape=(
-            shape(FIELDS, lines, cells),
             shape(36, lines, cells),
             shape(FIELDS, lines, cells),
             shape(80, cells),
@@ -397,8 +457,8 @@
             shape(HALF, cells),
             shape(36 * (levels + 1), lines, cells),
         ),
-        in_specs=[HBM] * 9,
-        out_specs=(VMEM,) * 7,
+        in_specs=[VMEM] * 2 + [HBM] * 8,
+        out_specs=(VMEM,) * 6,
         scratch_shapes=[
             pltpu.VMEM((FIELDS, lines, cells), jnp.float32),
             pltpu.VMEM((lines, cells), jnp.float32),
@@ -408,13 +468,14 @@
             pltpu.VMEM((36, lines, cells), jnp.float32),
             pltpu.VMEM((1, cells), jnp.int32),
             pltpu.VMEM((1, cells), jnp.int32),
-            pltpu.SemaphoreType.DMA((9,)),
+            pltpu.SemaphoreType.DMA((8,)),
         ],
     )(
+        flow,
+        halo,
         *(
-            pltpu.with_memory_space_constraint(x, pltpu.HBM)
+            in_hbm(x)
             for x in (
-                flow_state.reshape(FIELDS, lines, cells),
                 old_state.reshape(FIELDS, lines, cells),
                 local_step.reshape(lines, cells),
                 azim_flux,
@@ -424,44 +485,52 @@
                 intersection_first,
                 intersection_weight,
             )
-        )
+        ),
     )
-    ring_a = ring_b = upstream[:, :, axial - 2 :, :].reshape(FIELDS * HALF, cells)
-    at, mask = 0, sectors // 2
-    while mask:
-        from_a = flags[at : at + 1] != 0
-        from_b = flags[at + 1 : at + 2] != 0
-        sent = jnp.concatenate([jnp.where(from_a, ring_a, ring_b), ring], axis=0)
-        arrived = lax.ppermute(sent, "azim", [(i, i ^ mask) for i in range(sectors)])
-        upper = arrived[: FIELDS * HALF]
-        ring_a = jnp.where(from_a, upper, ring_a)
-        ring_b = jnp.where(from_b, upper, ring_b)
-        ring = jnp.concatenate([ring, arrived[FIELDS * HALF :]], axis=0)
-        at, mask = at + 2, mask // 2
-    ring = ring.reshape(sectors, HALF, cells)
+    ring_a = jnp.where(flags[0:1] != 0, upstream_far, upstream)
+    ring_b = jnp.where(flags[1:2] != 0, upstream_far, upstream)
+    ring = jnp.concatenate([packed, halo_far], axis=0)
+    at = 2
+    for masks in groups(sectors):
+        on_a, on_b, to_a = (flags[at + k : at + k + 1] for k in range(3))
+        arrived = [
+            exchange(
+                jnp.concatenate([jnp.where(to_a == mask, ring_a, ring_b), ring], axis=0), sectors, mask
+            )
+            for mask in masks
+        ]
+        for mask, values in zip(masks, arrived):
+            ring_a = jnp.where(on_a == mask, values[:count], ring_a)
+            ring_b = jnp.where(on_b == mask, values[:count], ring_b)
+        ring = jnp.concatenate([ring] + [values[count:] for values in arrived], axis=0)
+        at += 3
+    ring = ring.reshape(top, 2, HALF, cells)
+    halos = ring.reshape(sectors, HALF, cells)
 
     sweep, ends = call(
         functools.partial(source_kernel, sectors, levels),
         out_shape=(shape(FIELDS, lines, cells), shape(end_rows, cells)),
         in_specs=[VMEM] * 9,
         out_specs=(VMEM, VMEM),
-    )(ring_a, ring_b, ring, flow, gain, source, coef, flags, scan)
+    )(ring_a, ring_b, halos, flow, gain, source, coef, flags, scan)
+    values = exchange(jnp.concatenate([ends, ring[:, 0].reshape(top * HALF, cells)], axis=0), sectors, top)
+    ends = ends + values[:end_rows]
+    maps = jnp.concatenate([ring[:, 0], values[end_rows:].reshape(top, HALF, cells)], axis=0)
     suffix, closing = call(
         functools.partial(closing_kernel, sectors),
         out_shape=(shape(36, HALF, LANES), shape(36, HALF, LANES)),
         in_specs=[VMEM],
         out_specs=(VMEM, VMEM),
-    )(ring)
-    mask = 1
-    while mask < sectors:
-        ends = ends + lax.ppermute(ends, "azim", [(i, i ^ mask) for i in range(sectors)])
-        mask *= 2
+    )(maps)
+    for masks in groups(sectors):
+        for values in [exchange(ends, sectors, mask) for mask in masks]:
+            ends = ends + values
     new_state = call(
         functools.partial(finish_kernel, sectors, levels),
         out_shape=shape(FIELDS, lines, cells),
         in_specs=[VMEM] * 6,
         out_specs=VMEM,
-    )(ends, suffix, closing, flow, scan[36 * levels :], sweep)
+    )(ends, suffix, closing, flow, scan, sweep)
     return new_state.reshape(flow_state.shape)
 
 

time: 31.8 us -> 31 us (0.975)
  starting transfers between devices: 14.5 us -> 13.5 us
  Pallas kernels: 5.03 us -> 5.93 us
  waiting for transfers between devices: 11.9 us -> 11.2 us
    ppermute x7 -> x10, starting transfers between devices: 14.5 us -> 13.5 us  [the longest x8 8.33 us: exchange(): return lax.ppermute(values, 'azim', [(i, i ^ mask) for i in range(sectors)])]
    pallas_call x0 -> x1, Pallas kernels: none -> 0.9 us  [shards(): call(edges_kernel, out_shape=(shape(FIELDS, lines, cells), shape(count, c...]
    ppermute x7 -> x10, waiting for transfers between devices: 11.9 us -> 11.2 us  [the longest x8 11.2 us: exchange(): return lax.ppermute(values, 'azim', [(i, i ^ mask) for i in range(sectors)])]
  transfers between devices with their start and end apart: 7 -> 10, of which waited for: 7 -> 6; matrix products, arithmetic and copies ran while one was open for 0% -> 0% of each run, Pallas kernels for 9% -> 10%
where the time goes in v1:
time: 31 us; the launch traced here: 30.8 us
  starting transfers between devices  13.5 us (44%)
  waiting for transfers between devices  11.2 us (36%)
  Pallas kernels  5.93 us (19%)
    ppermute x8, waiting for transfers between devices, exchange(): return lax.ppermute(values, 'azim', [(i, i ^ mask) for i in range(sectors)])  11.2 us
    ppermute x8, starting transfers between devices, exchange(): return lax.ppermute(values, 'azim', [(i, i ^ mask) for i in range(sectors)])  8.33 us
    ppermute x2, starting transfers between devices, from_upstream(): lax.ppermute(values, ('azim', 'row'), [(i * row_count + r, (i ^ mask) * r...  5.16 us
    pallas_call x1, Pallas kernels, shards(): call(functools.partial(prepare_kernel, sectors, levels), out_shape=(shape...  2.41 us
    pallas_call x1, Pallas kernels, shards(): call(functools.partial(source_kernel, sectors, levels), out_shape=(shape(...  1.03 us
    pallas_call x1, Pallas kernels, shards(): call(functools.partial(finish_kernel, sectors, levels), out_shape=shape(F...  1.02 us
    pallas_call x1, Pallas kernels, shards(): call(edges_kernel, out_shape=(shape(FIELDS, lines, cells), shape(count, c...  0.9 us
  transfers between devices with their start and end apart: 10, of which 6 were waited for; matrix products, arithmetic and copies ran while one was open for 0% of the time, Pallas kernels for 10%

profile of v1, /device:TPU:0, one launch (start us, length us, event | category | flops | bytes accessed | tf_op | source)
XLA Modules:
  0.0 30.8 jit_solution(4754175397380695704)
XLA Ops:
  0.0 0.9 %shard_map.91 = (f32[6,16,128]{2,1,0:T(8,128)S(1)}, f32[48,128]{1,0:T(8,128)S(1)}, f32[8,128]{1,0:T(8,128)S(1)}) custom-call(f32[6,16,128]{2,1,0:T(8,128)} %bitcast.43), custom_call_target="tpu_custom_call" | custom-call | tf_op jit(solution)/shard_map/pallas_call | solution.py:439
  0.9 3.6 %collective-permute-start = (f32[48,128]{1,0:T(8,128)S(1)}, f32[48,128]{1,0:T(8,128)S(1)}, u32[]{:S(2)}, u32[]{:S(2)}) collective-permute-start(f32[48,128]{1,0:T(8,128)S(1)} %get-tuple-element.21), channel_id=1, source_target_pairs={{0,17},{1,18},{2,19},{3,16},{4,21},{5,22},{6,23},{7,20},{8,25},{9,... | collective-permute-start | bytes 73736 | tf_op jit(solution)/shard_map/ppermute | solution.py:397
  4.5 1.6 %collective-permute-start.1 = (f32[48,128]{1,0:T(8,128)S(1)}, f32[48,128]{1,0:T(8,128)S(1)}, u32[]{:S(2)}, u32[]{:S(2)}) collective-permute-start(f32[48,128]{1,0:T(8,128)S(1)} %get-tuple-element.21), channel_id=1, source_target_pairs={{0,1},{1,2},{2,3},{3,0},{4,5},{5,6},{6,7},{7,4},{8,9},{9,10},{10,1... | collective-permute-start | bytes 73736 | tf_op jit(solution)/shard_map/ppermute | solution.py:397
  6.1 0.3 %collective-permute-start.2 = (f32[8,128]{1,0:T(8,128)S(1)}, f32[8,128]{1,0:T(8,128)S(1)}, u32[]{:S(2)}, u32[]{:S(2)}) collective-permute-start(f32[8,128]{1,0:T(8,128)S(1)} %get-tuple-element.19.halo), channel_id=1, source_target_pairs={{0,16},{4,20},{8,24},{12,28},{16,0},{20,4},{24,8},{28,12},{1,17},{... | collective-permute-start | bytes 12296 | tf_op jit(solution)/shard_map/ppermute | solution.py:393
  6.4 2.4 %shard_map.92 = (f32[36,16,128]{2,1,0:T(8,128)S(1)}, f32[6,16,128]{2,1,0:T(8,128)S(1)}, f32[80,128]{1,0:T(8,128)S(1)}, s32[16,128]{1,0:T(8,128)S(1)}, f32[8,128]{1,0:T(8,128)S(1)}, /*index=5*/f32[288,16,128]{2,1,0:T(8,128)S(1)}) custom-call(f32[6,16,128]{2,1,0:T(8,128)S(1)} %get-tuple-element.18.flow, f32[8,128]{1,0:T(8,128)S(1)} %get-tuple-element.19.halo, ...), custom_call_target="tpu_custom_call" | custom-call | tf_op jit(solution)/shard_map/pallas_call | solution.py:450
  8.9 0.0 collective-permute-done
  8.9 0.0 collective-permute-done.1
  8.9 1.7 %collective-permute-done.2 = f32[8,128]{1,0:T(8,128)S(1)} collective-permute-done((f32[8,128]{1,0:T(8,128)S(1)}, f32[8,128]{1,0:T(8,128)S(1)}, u32[]{:S(2)}, u32[]{:S(2)}) %collective-permute-start.2) | collective-permute-done | bytes 4128 | tf_op jit(solution)/shard_map/ppermute | solution.py:393
  10.6 1.6 %collective-permute-start.5 = (f32[64,128]{1,0:T(8,128)S(1)}, f32[64,128]{1,0:T(8,128)S(1)}, u32[]{:S(2)}, u32[]{:S(2)}) collective-permute-start(f32[64,128]{1,0:T(8,128)S(1)} %get-tuple-element.53), channel_id=1, source_target_pairs={{0,4},{4,0},{8,12},{12,8},{16,20},{20,16},{24,28},{28,24},{1,5},{5... | collective-permute-start | bytes 98312 | tf_op jit(solution)/shard_map/ppermute | solution.py:393
  12.2 1.6 %collective-permute-start.4 = (f32[64,128]{1,0:T(8,128)S(1)}, f32[64,128]{1,0:T(8,128)S(1)}, u32[]{:S(2)}, u32[]{:S(2)}) collective-permute-start(f32[64,128]{1,0:T(8,128)S(1)} %get-tuple-element.52), channel_id=1, source_target_pairs={{0,8},{4,12},{8,0},{12,4},{16,24},{20,28},{24,16},{28,20},{1,9},{5... | collective-permute-start | bytes 98312 | tf_op jit(solution)/shard_map/ppermute | solution.py:393
  13.8 0.4 %collective-permute-start.3 = (f32[64,128]{1,0:T(8,128)S(1)}, f32[64,128]{1,0:T(8,128)S(1)}, u32[]{:S(2)}, u32[]{:S(2)}) collective-permute-start(f32[64,128]{1,0:T(8,128)S(1)} %get-tuple-element.51), channel_id=1, source_target_pairs={{0,12},{4,8},{8,4},{12,0},{16,28},{20,24},{24,20},{28,16},{1,13},{... | collective-permute-start | bytes 98312 | tf_op jit(solution)/shard_map/ppermute | solution.py:393
  14.1 0.4 %collective-permute-done.5 = f32[64,128]{1,0:T(8,128)S(1)} collective-permute-done((f32[64,128]{1,0:T(8,128)S(1)}, f32[64,128]{1,0:T(8,128)S(1)}, u32[]{:S(2)}, u32[]{:S(2)}) %collective-permute-start.5) | collective-permute-done | bytes 32800 | tf_op jit(solution)/shard_map/ppermute | solution.py:393
  14.6 1.5 %collective-permute-done.4 = f32[64,128]{1,0:T(8,128)S(1)} collective-permute-done((f32[64,128]{1,0:T(8,128)S(1)}, f32[64,128]{1,0:T(8,128)S(1)}, u32[]{:S(2)}, u32[]{:S(2)}) %collective-permute-start.4) | collective-permute-done | bytes 32800 | tf_op jit(solution)/shard_map/ppermute | solution.py:393
  16.1 2.5 %collective-permute-done.3 = f32[64,128]{1,0:T(8,128)S(1)} collective-permute-done((f32[64,128]{1,0:T(8,128)S(1)}, f32[64,128]{1,0:T(8,128)S(1)}, u32[]{:S(2)}, u32[]{:S(2)}) %collective-permute-start.3) | collective-permute-done | bytes 32800 | tf_op jit(solution)/shard_map/ppermute | solution.py:393
  18.6 1.0 %shard_map.93 = (f32[6,16,128]{2,1,0:T(8,128)S(1)}, f32[8,128]{1,0:T(8,128)S(1)}) custom-call(f32[48,128]{1,0:T(8,128)S(1)} %get-tuple-element.35.ring_a, f32[48,128]{1,0:T(8,128)S(1)} %get-tuple-element.34.ring_b, f32[8,8,128]{2,1,0:T(8,128)S(1)} %bitcast.40, f32[6,16,128]{2,1,0:T(8,128)S(1)} %get-tuple-element.18.flow, ...), custom_call_target="tpu_custom_call" | custom-call | tf_op jit(solution)/shard_map/pallas_call | solution.py:510
  19.6 1.0 %collective-permute-start.6 = (f32[40,128]{1,0:T(8,128)S(1)}, f32[40,128]{1,0:T(8,128)S(1)}, u32[]{:S(2)}, u32[]{:S(2)}) collective-permute-start(f32[40,128]{1,0:T(8,128)S(1)} %pad_maximum_fusion.7), channel_id=1, source_target_pairs={{0,16},{4,20},{8,24},{12,28},{16,0},{20,4},{24,8},{28,12},{1,17},{... | collective-permute-start | bytes 61448 | tf_op jit(solution)/shard_map/ppermute | solution.py:393
  20.6 3.8 %collective-permute-done.6 = f32[40,128]{1,0:T(8,128)S(1)} collective-permute-done((f32[40,128]{1,0:T(8,128)S(1)}, f32[40,128]{1,0:T(8,128)S(1)}, u32[]{:S(2)}, u32[]{:S(2)}) %collective-permute-start.6) | collective-permute-done | bytes 20512 | tf_op jit(solution)/shard_map/ppermute | solution.py:393
  24.4 0.5 %collective-permute-start.7 = (f32[8,128]{1,0:T(8,128)S(1)}, f32[8,128]{1,0:T(8,128)S(1)}, u32[]{:S(2)}, u32[]{:S(2)}) collective-permute-start(f32[8,128]{1,0:T(8,128)S(1)} %slice_add_fusion), channel_id=1, source_target_pairs={{0,4},{4,0},{8,12},{12,8},{16,20},{20,16},{24,28},{28,24},{1,5},{5... | collective-permute-start | bytes 12296 | tf_op jit(solution)/shard_map/ppermute | solution.py:393
  24.9 0.3 %collective-permute-start.8 = (f32[8,128]{1,0:T(8,128)S(1)}, f32[8,128]{1,0:T(8,128)S(1)}, u32[]{:S(2)}, u32[]{:S(2)}) collective-permute-start(f32[8,128]{1,0:T(8,128)S(1)} %slice_add_fusion), channel_id=1, source_target_pairs={{0,8},{4,12},{8,0},{12,4},{16,24},{20,28},{24,16},{28,20},{1,9},{5... | collective-permute-start | bytes 12296 | tf_op jit(solution)/shard_map/ppermute | solution.py:393
  25.3 2.6 %collective-permute-start.9 = (f32[8,128]{1,0:T(8,128)S(1)}, f32[8,128]{1,0:T(8,128)S(1)}, u32[]{:S(2)}, u32[]{:S(2)}) collective-permute-start(f32[8,128]{1,0:T(8,128)S(1)} %slice_add_fusion), channel_id=1, source_target_pairs={{0,12},{4,8},{8,4},{12,0},{16,28},{20,24},{24,20},{28,16},{1,13},{... | collective-permute-start | bytes 12296 | tf_op jit(solution)/shard_map/ppermute | solution.py:393
  27.9 0.6 %shard_map.94 = (f32[36,8,128]{2,1,0:T(8,128)S(1)}, f32[36,8,128]{2,1,0:T(8,128)S(1)}) custom-call(f32[8,8,128]{2,1,0:T(8,128)S(1)} %pad_maximum_fusion.6.ring), custom_call_target="tpu_custom_call" | custom-call | tf_op jit(solution)/shard_map/pallas_call | solution.py:519
  28.5 0.0 collective-permute-done.7
  28.5 0.0 collective-permute-done.8
  28.6 1.2 %collective-permute-done.9 = f32[8,128]{1,0:T(8,128)S(1)} collective-permute-done((f32[8,128]{1,0:T(8,128)S(1)}, f32[8,128]{1,0:T(8,128)S(1)}, u32[]{:S(2)}, u32[]{:S(2)}) %collective-permute-start.9) | collective-permute-done | bytes 4128 | tf_op jit(solution)/shard_map/ppermute | solution.py:393
  29.8 1.0 %shard_map.95 = f32[6,16,128]{2,1,0:T(8,128)} custom-call(f32[8,128]{1,0:T(8,128)S(1)} %add_add_fusion.gathered, f32[36,8,128]{2,1,0:T(8,128)S(1)} %get-tuple-element.28.suffix, f32[36,8,128]{2,1,0:T(8,128)S(1)} %get-tuple-element.29.closing, f32[6,16,128]{2,1,0:T(8,128)S(1)} %get-tuple-element.18.flow, f32[288,16,128]{2,1,0:T(8,128)S(1)} %get-tuple-element.26.scan, ...), custom_call_target="tpu_custom_call" | custom-call | tf_op jit(solution)/shard_map/pallas_call | solution.py:528
  (16 shorter events, 0.1 us)
Async XLA Ops:
  0.9 7.9 %collective-permute-start = (f32[48,128]{1,0:T(8,128)S(1)}, f32[48,128]{1,0:T(8,128)S(1)}, u32[]{:S(2)}, u32[]{:S(2)}) collective-permute-start(f32[48,128]{1,0:T(8,128)S(1)} %get-tuple-element.21), channel_id=1, source_target_pairs={{0,17},{1,18},{2,19},{3,16},{4,21},{5,22},{6,23},{7,20},{8,25},{9,... | collective-permute-start | bytes 73736 | tf_op jit(solution)/shard_map/ppermute | solution.py:397
  4.5 4.4 %collective-permute-start.1 = (f32[48,128]{1,0:T(8,128)S(1)}, f32[48,128]{1,0:T(8,128)S(1)}, u32[]{:S(2)}, u32[]{:S(2)}) collective-permute-start(f32[48,128]{1,0:T(8,128)S(1)} %get-tuple-element.21), channel_id=1, source_target_pairs={{0,1},{1,2},{2,3},{3,0},{4,5},{5,6},{6,7},{7,4},{8,9},{9,10},{10,1... | collective-permute-start | bytes 73736 | tf_op jit(solution)/shard_map/ppermute | solution.py:397
  6.1 4.5 %collective-permute-start.2 = (f32[8,128]{1,0:T(8,128)S(1)}, f32[8,128]{1,0:T(8,128)S(1)}, u32[]{:S(2)}, u32[]{:S(2)}) collective-permute-start(f32[8,128]{1,0:T(8,128)S(1)} %get-tuple-element.19.halo), channel_id=1, source_target_pairs={{0,16},{4,20},{8,24},{12,28},{16,0},{20,4},{24,8},{28,12},{1,17},{... | collective-permute-start | bytes 12296 | tf_op jit(solution)/shard_map/ppermute | solution.py:393
  10.6 4.0 %collective-permute-start.5 = (f32[64,128]{1,0:T(8,128)S(1)}, f32[64,128]{1,0:T(8,128)S(1)}, u32[]{:S(2)}, u32[]{:S(2)}) collective-permute-start(f32[64,128]{1,0:T(8,128)S(1)} %get-tuple-element.53), channel_id=1, source_target_pairs={{0,4},{4,0},{8,12},{12,8},{16,20},{20,16},{24,28},{28,24},{1,5},{5... | collective-permute-start | bytes 98312 | tf_op jit(solution)/shard_map/ppermute | solution.py:393
  12.2 3.9 %collective-permute-start.4 = (f32[64,128]{1,0:T(8,128)S(1)}, f32[64,128]{1,0:T(8,128)S(1)}, u32[]{:S(2)}, u32[]{:S(2)}) collective-permute-start(f32[64,128]{1,0:T(8,128)S(1)} %get-tuple-element.52), channel_id=1, source_target_pairs={{0,8},{4,12},{8,0},{12,4},{16,24},{20,28},{24,16},{28,20},{1,9},{5... | collective-permute-start | bytes 98312 | tf_op jit(solution)/shard_map/ppermute | solution.py:393
  13.8 4.8 %collective-permute-start.3 = (f32[64,128]{1,0:T(8,128)S(1)}, f32[64,128]{1,0:T(8,128)S(1)}, u32[]{:S(2)}, u32[]{:S(2)}) collective-permute-start(f32[64,128]{1,0:T(8,128)S(1)} %get-tuple-element.51), channel_id=1, source_target_pairs={{0,12},{4,8},{8,4},{12,0},{16,28},{20,24},{24,20},{28,16},{1,13},{... | collective-permute-start | bytes 98312 | tf_op jit(solution)/shard_map/ppermute | solution.py:393
  19.6 4.8 %collective-permute-start.6 = (f32[40,128]{1,0:T(8,128)S(1)}, f32[40,128]{1,0:T(8,128)S(1)}, u32[]{:S(2)}, u32[]{:S(2)}) collective-permute-start(f32[40,128]{1,0:T(8,128)S(1)} %pad_maximum_fusion.7), channel_id=1, source_target_pairs={{0,16},{4,20},{8,24},{12,28},{16,0},{20,4},{24,8},{28,12},{1,17},{... | collective-permute-start | bytes 61448 | tf_op jit(solution)/shard_map/ppermute | solution.py:393
  24.4 4.1 %collective-permute-start.7 = (f32[8,128]{1,0:T(8,128)S(1)}, f32[8,128]{1,0:T(8,128)S(1)}, u32[]{:S(2)}, u32[]{:S(2)}) collective-permute-start(f32[8,128]{1,0:T(8,128)S(1)} %slice_add_fusion), channel_id=1, source_target_pairs={{0,4},{4,0},{8,12},{12,8},{16,20},{20,16},{24,28},{28,24},{1,5},{5... | collective-permute-start | bytes 12296 | tf_op jit(solution)/shard_map/ppermute | solution.py:393
  24.9 3.6 %collective-permute-start.8 = (f32[8,128]{1,0:T(8,128)S(1)}, f32[8,128]{1,0:T(8,128)S(1)}, u32[]{:S(2)}, u32[]{:S(2)}) collective-permute-start(f32[8,128]{1,0:T(8,128)S(1)} %slice_add_fusion), channel_id=1, source_target_pairs={{0,8},{4,12},{8,0},{12,4},{16,24},{20,28},{24,16},{28,20},{1,9},{5... | collective-permute-start | bytes 12296 | tf_op jit(solution)/shard_map/ppermute | solution.py:393
  25.3 4.5 %collective-permute-start.9 = (f32[8,128]{1,0:T(8,128)S(1)}, f32[8,128]{1,0:T(8,128)S(1)}, u32[]{:S(2)}, u32[]{:S(2)}) collective-permute-start(f32[8,128]{1,0:T(8,128)S(1)} %slice_add_fusion), channel_id=1, source_target_pairs={{0,12},{4,8},{8,4},{12,0},{16,28},{20,24},{24,20},{28,16},{1,13},{... | collective-permute-start | bytes 12296 | tf_op jit(solution)/shard_map/ppermute | solution.py:393

commit v2 on v1

--- a/solution.py
+++ b/solution.py
@@ -234,9 +234,7 @@
     return gathered_at(sectors, difference) + (difference // (sectors // 2)) * (sectors // 2)
 
 
-def source_kernel(
-    sectors, levels, ring_a, ring_b, ring, flow, gain, source, coef, flags, scan, sweep, packed
-):
+def residual_kernel(sectors, ring_a, ring_b, ring, flow, coef, flags, reach, base, residual_out, packed):
     lane = lane_ids()
     sub = lax.broadcasted_iota(jnp.int32, (HALF, LANES), 0)
     place = lax.axis_index("azim")
@@ -259,6 +257,7 @@
         ghost.append(frac * one + (1.0 - frac) * two)
     halo = jnp.where((lane & 3) < 2, right_pack, left_pack)
     axial = sub % 4
+    ends = [[None, None] for _ in range(FIELDS)]
     is_first_row = row == 0
     for half in range(2):
         u0 = [flow[f, rows(half), :] for f in range(FIELDS)]
@@ -296,38 +295,77 @@
                 at = f * FIELDS + g
                 acc = acc + coefficient(at) * az_central[g] + coefficient(36 + at) * ax_central[g]
             residual.append(acc)
-        added = matvec([gain[e, rows(half), :] for e in range(36)], residual)
         for f in range(FIELDS):
-            sweep[f, rows(half), :] = source[f, rows(half), :] + added[f]
-    values = [[sweep[f, rows(half), :] for half in range(2)] for f in range(FIELDS)]
+            residual_out[f, rows(half), :] = residual[f]
+        parts = matvec([reach[e, rows(half), :] for e in range(36)], residual)
+        for f in range(FIELDS):
+            ends[f][half] = jnp.sum(parts[f], axis=1, keepdims=True)
+    per = packing(sectors)
+    for first in range(0, FIELDS, per):
+        acc = base[pl.ds(HALF * (first // per), HALF), :]
+        for entry, pair in enumerate(ends[first : first + per]):
+            for half in range(2):
+                target = entry * 2 * sectors + half
+                acc = jnp.where(lane == target, acc + jnp.broadcast_to(pair[half], (HALF, LANES)), acc)
+        packed[pl.ds(HALF * (first // per), HALF), :] = roll_lanes(acc, 2 * place)
+
+
+def reach_kernel(sectors, levels, scan, gain, source, reach, base, work):
+    lane = lane_ids()
+    one = [jnp.float32(1.0 if e % 7 == 0 else 0.0) for e in range(36)]
+    for half in range(2):
+        for e in range(36):
+            work[e, rows(half), :] = scan[e, rows(half), :]
+    for level in range(levels):
+        step = 1 << level
+        for half in range(2):
+            here = [work[e, rows(half), :] for e in range(36)]
+            later = [
+                jnp.where(lane < LANES - step, roll_lanes(x, -step), one[e]) for e, x in enumerate(here)
+            ]
+            for e, value in enumerate(product(later, here)):
+                work[e, rows(half), :] = value
+    sums = [[None, None] for _ in range(FIELDS)]
+    for half in range(2):
+        after = [
+            jnp.where(lane < LANES - 1, roll_lanes(work[e, rows(half), :], -1), one[e]) for e in range(36)
+        ]
+        for e, value in enumerate(product(after, [gain[e, rows(half), :] for e in range(36)])):
+            reach[e, rows(half), :] = value
+        for f, value in enumerate(matvec(after, [source[f, rows(half), :] for f in range(FIELDS)])):
+            sums[f][half] = jnp.sum(value, axis=1, keepdims=True)
+    per = packing(sectors)
+    for first in range(0, FIELDS, per):
+        acc = jnp.zeros((HALF, LANES), jnp.float32)
+        for entry, pair in enumerate(sums[first : first + per]):
+            for half in range(2):
+                target = entry * 2 * sectors + half
+                acc = jnp.where(lane == target, jnp.broadcast_to(pair[half], (HALF, LANES)), acc)
+        base[pl.ds(HALF * (first // per), HALF), :] = acc
+
+
+def sweep_kernel(levels, residual, gain, source, scan, sweep):
+    lane = lane_ids()
+    values = [[None, None] for _ in range(FIELDS)]
+    for half in range(2):
+        added = matvec(
+            [gain[e, rows(half), :] for e in range(36)], [residual[f, rows(half), :] for f in range(FIELDS)]
+        )
+        for f in range(FIELDS):
+            values[f][half] = source[f, rows(half), :] + added[f]
     for level in range(levels):
         step = 1 << level
         for half in range(2):
             before = [jnp.where(lane < step, 0.0, roll_lanes(values[f][half], step)) for f in range(FIELDS)]
             matrix = [scan[36 * level + e, rows(half), :] for e in range(36)]
-            for f, gain in enumerate(matvec(matrix, before)):
-                values[f][half] = values[f][half] + gain
+            for f, gained in enumerate(matvec(matrix, before)):
+                values[f][half] = values[f][half] + gained
     for f in range(FIELDS):
         for half in range(2):
             sweep[f, rows(half), :] = values[f][half]
-    per = packing(sectors)
-    for at in range(0, FIELDS, per):
-        value = pack_last_lane(values[at : at + per], lane, 0, 2 * sectors)
-        packed[pl.ds(HALF * (at // per), HALF), :] = roll_lanes(value, 2 * place)
-
-
-def relative(pack, entry, sectors, place, lane):
-    per = packing(sectors)
-    width = 2 * sectors
-    base = (entry % per) * width
-    row = pack[pl.ds(HALF * (entry // per), HALF), :]
-    turn = 2 * place
-    here = pltpu.roll(row, lax.rem(2 * LANES - base - turn, LANES), 1)
-    wrapped = pltpu.roll(row, lax.rem(2 * LANES - base - turn + width, LANES), 1)
-    return jnp.where(lane < width - turn, here, wrapped)
-
-
-def closing_kernel(sectors, ring, suffix, closing):
+
+
+def closing_kernel(sectors, ring, weights):
     lane = lane_ids()
     place = lax.axis_index("azim")
     width = 2 * sectors
@@ -348,8 +386,7 @@
         later = [jnp.where(lane < width - step, roll_lanes(x, -step), one[e]) for e, x in enumerate(maps)]
         maps = product(later, maps)
         step *= 2
-    for e in range(36):
-        suffix[e] = jnp.where(lane < width - 2, roll_lanes(maps[e], -2), one[e])
+    suffix = [jnp.where(lane < width - 2, roll_lanes(maps[e], -2), one[e]) for e in range(36)]
     system = [[one[f * 6 + g] - maps[f * 6 + g] for g in range(6)] for f in range(6)]
     result = [[jnp.full((HALF, LANES), one[f * 6 + g]) for g in range(6)] for f in range(6)]
     for pivot in range(6):
@@ -366,27 +403,47 @@
                 system[f][g] = system[f][g] - factor * system[pivot][g]
             for g in range(pivot + 1):
                 result[f][g] = result[f][g] - factor * result[pivot][g]
-    for f in range(6):
-        for g in range(6):
-            closing[f * 6 + g] = result[f][g]
-
-
-def finish_kernel(sectors, levels, gathered, suffix, closing, flow, scan, sweep, out):
+    closing = []
+    for e in range(36):
+        value = jnp.where(lane < 2, result[e // 6][e % 6], 0.0)
+        step = 2
+        while step < width:
+            value = value + roll_lanes(value, step)
+            step *= 2
+        closing.append(value)
+    start = product(closing, suffix)
+    per = packing(sectors)
+    turn = 2 * place
+    crossed = (lane & (width - 1)) < turn
+    for f in range(FIELDS):
+        for first in range(0, FIELDS, per):
+            acc = jnp.zeros((HALF, LANES), jnp.float32)
+            for entry in range(min(per, FIELDS - first)):
+                at = entry * width
+                inside = (lane >= at) & (lane < at + width)
+                acc = jnp.where(inside, roll_lanes(start[f * 6 + first + entry], at), acc)
+            ahead = pltpu.roll(acc, turn, 1)
+            behind = pltpu.roll(acc, lax.rem(LANES + turn - width, LANES), 1)
+            row = HALF * (f * pl.cdiv(FIELDS, per) + first // per)
+            weights[pl.ds(row, HALF), :] = jnp.where(crossed, behind, ahead)
+
+
+def finish_kernel(sectors, levels, gathered, weights, flow, scan, sweep, out):
     lane = lane_ids()
-    place = lax.axis_index("azim")
-    width = 2 * sectors
-    ends = [relative(gathered, f, sectors, place, lane) for f in range(FIELDS)]
-    total = matvec([suffix[e] for e in range(36)], ends)
-    step = width // 2
-    while step >= 2:
-        total = [x + roll_lanes(x, -step) for x in total]
-        step //= 2
-    start = matvec([closing[e] for e in range(36)], total)
+    count = pl.cdiv(FIELDS, packing(sectors))
+    begin = [[None] * FIELDS for _ in range(2)]
+    for f in range(FIELDS):
+        acc = None
+        for at in range(count):
+            term = weights[pl.ds(HALF * (f * count + at), HALF), :] * gathered[pl.ds(HALF * at, HALF), :]
+            acc = term if acc is None else acc + term
+        for half in range(2):
+            total = jnp.sum(jnp.where((lane & 1) == half, acc, 0.0), axis=1, keepdims=True)
+            begin[half][f] = jnp.broadcast_to(total, (HALF, LANES))
     for half in range(2):
-        begin = [jnp.broadcast_to(x[:, half : half + 1], (HALF, LANES)) for x in start]
-        gain = matvec([scan[36 * levels + e, rows(half), :] for e in range(36)], begin)
+        gained = matvec([scan[36 * levels + e, rows(half), :] for e in range(36)], begin[half])
         for f in range(FIELDS):
-            out[f, rows(half), :] = flow[f, rows(half), :] + (gain[f] + sweep[f, rows(half), :])
+            out[f, rows(half), :] = flow[f, rows(half), :] + (gained[f] + sweep[f, rows(half), :])
 
 
 def exchange(values, sectors, mask):
@@ -493,12 +550,10 @@
     at = 2
     for masks in groups(sectors):
         on_a, on_b, to_a = (flags[at + k : at + k + 1] for k in range(3))
-        arrived = [
-            exchange(
-                jnp.concatenate([jnp.where(to_a == mask, ring_a, ring_b), ring], axis=0), sectors, mask
-            )
-            for mask in masks
-        ]
+        arrived = []
+        for mask in masks:
+            sent = jnp.concatenate([jnp.where(to_a == mask, ring_a, ring_b), ring], axis=0)
+            arrived.append(exchange(sent, sectors, mask))
         for mask, values in zip(masks, arrived):
             ring_a = jnp.where(on_a == mask, values[:count], ring_a)
             ring_b = jnp.where(on_b == mask, values[:count], ring_b)
@@ -507,20 +562,34 @@
     ring = ring.reshape(top, 2, HALF, cells)
     halos = ring.reshape(sectors, HALF, cells)
 
-    sweep, ends = call(
-        functools.partial(source_kernel, sectors, levels),
+    reach, base = call(
+        functools.partial(reach_kernel, sectors, levels),
+        out_shape=(shape(36, lines, cells), shape(end_rows, cells)),
+        in_specs=[VMEM] * 3,
+        out_specs=(VMEM, VMEM),
+        scratch_shapes=[pltpu.VMEM((36, lines, cells), jnp.float32)],
+    )(scan, gain, source)
+    residual, ends = call(
+        functools.partial(residual_kernel, sectors),
         out_shape=(shape(FIELDS, lines, cells), shape(end_rows, cells)),
-        in_specs=[VMEM] * 9,
+        in_specs=[VMEM] * 8,
         out_specs=(VMEM, VMEM),
-    )(ring_a, ring_b, halos, flow, gain, source, coef, flags, scan)
+    )(ring_a, ring_b, halos, flow, coef, flags, reach, base)
+    sweep = call(
+        functools.partial(sweep_kernel, levels),
+        out_shape=shape(FIELDS, lines, cells),
+        in_specs=[VMEM] * 4,
+        out_specs=VMEM,
+        cost_estimate=pl.CostEstimate(flops=1 << 20, bytes_accessed=1 << 21, transcendentals=0),
+    )(residual, gain, source, scan)
     values = exchange(jnp.concatenate([ends, ring[:, 0].reshape(top * HALF, cells)], axis=0), sectors, top)
     ends = ends + values[:end_rows]
     maps = jnp.concatenate([ring[:, 0], values[end_rows:].reshape(top, HALF, cells)], axis=0)
-    suffix, closing = call(
+    weights = call(
         functools.partial(closing_kernel, sectors),
-        out_shape=(shape(36, HALF, LANES), shape(36, HALF, LANES)),
+        out_shape=shape(FIELDS * end_rows, cells),
         in_specs=[VMEM],
-        out_specs=(VMEM, VMEM),
+        out_specs=VMEM,
     )(maps)
     for masks in groups(sectors):
         for values in [exchange(ends, sectors, mask) for mask in masks]:
@@ -528,9 +597,9 @@
     new_state = call(
         functools.partial(finish_kernel, sectors, levels),
         out_shape=shape(FIELDS, lines, cells),
-        in_specs=[VMEM] * 6,
+        in_specs=[VMEM] * 5,
         out_specs=VMEM,
-    )(ends, suffix, closing, flow, scan, sweep)
+    )(ends, weights, flow, scan, sweep)
     return new_state.reshape(flow_state.shape)
 
 

time: 31 us -> 30.1 us (0.971)
  waiting for transfers between devices: 11.2 us -> 8.02 us
  Pallas kernels: 5.93 us -> 7.14 us
  starting transfers between devices: 13.5 us -> 14.6 us
    ppermute x8, waiting for transfers between devices: 11.2 us -> 8.02 us  [exchange(): return lax.ppermute(values, 'azim', [(i, i ^ mask) for i in range(sectors)])]
    pallas_call x2 -> x4, Pallas kernels: 1.6 us -> 3.1 us  [the longest x1 1.12 us: shards(): call(functools.partial(reach_kernel, sectors, levels), out_shape=(shape(3...]
    ppermute x8, starting transfers between devices: 8.33 us -> 9.44 us  [exchange(): return lax.ppermute(values, 'azim', [(i, i ^ mask) for i in range(sectors)])]
  transfers between devices with their start and end apart: 10 -> 10, of which waited for: 6 -> 6; matrix products, arithmetic and copies ran while one was open for 0% -> 0% of each run, Pallas kernels for 10% -> 17%
where the time goes in v2:
time: 30.1 us; the launch traced here: 30 us
  starting transfers between devices  14.6 us (49%)
  waiting for transfers between devices  8.02 us (27%)
  Pallas kernels  7.14 us (24%)
    ppermute x8, starting transfers between devices, exchange(): return lax.ppermute(values, 'azim', [(i, i ^ mask) for i in range(sectors)])  9.44 us
    ppermute x8, waiting for transfers between devices, exchange(): return lax.ppermute(values, 'azim', [(i, i ^ mask) for i in range(sectors)])  8.02 us
    ppermute x2, starting transfers between devices, from_upstream(): lax.ppermute(values, ('azim', 'row'), [(i * row_count + r, (i ^ mask) * r...  5.16 us
    pallas_call x1, Pallas kernels, shards(): call(functools.partial(prepare_kernel, sectors, levels), out_shape=(shape...  2.41 us
    pallas_call x1, Pallas kernels, shards(): call(functools.partial(reach_kernel, sectors, levels), out_shape=(shape(3...  1.12 us
    pallas_call x1, Pallas kernels, shards(): call(functools.partial(closing_kernel, sectors), out_shape=shape(FIELDS *...  0.93 us
    pallas_call x1, Pallas kernels, shards(): call(edges_kernel, out_shape=(shape(FIELDS, lines, cells), shape(count, c...  0.9 us
    pallas_call x1, Pallas kernels, shards(): call(functools.partial(finish_kernel, sectors, levels), out_shape=shape(F...  0.73 us
  transfers between devices with their start and end apart: 10, of which 6 were waited for; matrix products, arithmetic and copies ran while one was open for 0% of the time, Pallas kernels for 17%

profile of v2, /device:TPU:0, one launch (start us, length us, event | category | flops | bytes accessed | tf_op | source)
XLA Modules:
  0.0 30.0 jit_solution(11721426044756959935)
XLA Ops:
  0.0 0.9 %shard_map.91 = (f32[6,16,128]{2,1,0:T(8,128)S(1)}, f32[48,128]{1,0:T(8,128)S(1)}, f32[8,128]{1,0:T(8,128)S(1)}) custom-call(f32[6,16,128]{2,1,0:T(8,128)} %bitcast.43), custom_call_target="tpu_custom_call" | custom-call | tf_op jit(solution)/shard_map/pallas_call | solution.py:496
  0.9 3.6 %collective-permute-start = (f32[48,128]{1,0:T(8,128)S(1)}, f32[48,128]{1,0:T(8,128)S(1)}, u32[]{:S(2)}, u32[]{:S(2)}) collective-permute-start(f32[48,128]{1,0:T(8,128)S(1)} %get-tuple-element.21), channel_id=1, source_target_pairs={{0,17},{1,18},{2,19},{3,16},{4,21},{5,22},{6,23},{7,20},{8,25},{9,... | collective-permute-start | bytes 73736 | tf_op jit(solution)/shard_map/ppermute | solution.py:454
  4.5 1.6 %collective-permute-start.1 = (f32[48,128]{1,0:T(8,128)S(1)}, f32[48,128]{1,0:T(8,128)S(1)}, u32[]{:S(2)}, u32[]{:S(2)}) collective-permute-start(f32[48,128]{1,0:T(8,128)S(1)} %get-tuple-element.21), channel_id=1, source_target_pairs={{0,1},{1,2},{2,3},{3,0},{4,5},{5,6},{6,7},{7,4},{8,9},{9,10},{10,1... | collective-permute-start | bytes 73736 | tf_op jit(solution)/shard_map/ppermute | solution.py:454
  6.1 0.3 %collective-permute-start.2 = (f32[8,128]{1,0:T(8,128)S(1)}, f32[8,128]{1,0:T(8,128)S(1)}, u32[]{:S(2)}, u32[]{:S(2)}) collective-permute-start(f32[8,128]{1,0:T(8,128)S(1)} %get-tuple-element.19.halo), channel_id=1, source_target_pairs={{0,16},{4,20},{8,24},{12,28},{16,0},{20,4},{24,8},{28,12},{1,17},{... | collective-permute-start | bytes 12296 | tf_op jit(solution)/shard_map/ppermute | solution.py:450
  6.4 2.4 %shard_map.92 = (f32[36,16,128]{2,1,0:T(8,128)S(1)}, f32[6,16,128]{2,1,0:T(8,128)S(1)}, f32[80,128]{1,0:T(8,128)S(1)}, s32[16,128]{1,0:T(8,128)S(1)}, f32[8,128]{1,0:T(8,128)S(1)}, /*index=5*/f32[288,16,128]{2,1,0:T(8,128)S(1)}) custom-call(f32[6,16,128]{2,1,0:T(8,128)S(1)} %get-tuple-element.18.flow, f32[8,128]{1,0:T(8,128)S(1)} %get-tuple-element.19.halo, ...), custom_call_target="tpu_custom_call" | custom-call | tf_op jit(solution)/shard_map/pallas_call | solution.py:507
  8.9 1.1 %shard_map.93 = (f32[36,16,128]{2,1,0:T(8,128)S(1)}, f32[8,128]{1,0:T(8,128)S(1)}) custom-call(f32[288,16,128]{2,1,0:T(8,128)S(1)} %get-tuple-element.24.scan, f32[36,16,128]{2,1,0:T(8,128)S(1)} %get-tuple-element.25.gain, f32[6,16,128]{2,1,0:T(8,128)S(1)} %get-tuple-element.26.source), custom_call_target="tpu_custom_call" | custom-call | tf_op jit(solution)/shard_map/pallas_call | solution.py:565
  10.0 0.0 collective-permute-done
  10.0 0.0 collective-permute-done.1
  10.0 0.6 %collective-permute-done.2 = f32[8,128]{1,0:T(8,128)S(1)} collective-permute-done((f32[8,128]{1,0:T(8,128)S(1)}, f32[8,128]{1,0:T(8,128)S(1)}, u32[]{:S(2)}, u32[]{:S(2)}) %collective-permute-start.2) | collective-permute-done | bytes 4128 | tf_op jit(solution)/shard_map/ppermute | solution.py:450
  10.6 1.6 %collective-permute-start.5 = (f32[64,128]{1,0:T(8,128)S(1)}, f32[64,128]{1,0:T(8,128)S(1)}, u32[]{:S(2)}, u32[]{:S(2)}) collective-permute-start(f32[64,128]{1,0:T(8,128)S(1)} %get-tuple-element.53), channel_id=1, source_target_pairs={{0,4},{4,0},{8,12},{12,8},{16,20},{20,16},{24,28},{28,24},{1,5},{5... | collective-permute-start | bytes 98312 | tf_op jit(solution)/shard_map/ppermute | solution.py:450
  12.2 1.6 %collective-permute-start.4 = (f32[64,128]{1,0:T(8,128)S(1)}, f32[64,128]{1,0:T(8,128)S(1)}, u32[]{:S(2)}, u32[]{:S(2)}) collective-permute-start(f32[64,128]{1,0:T(8,128)S(1)} %get-tuple-element.52), channel_id=1, source_target_pairs={{0,8},{4,12},{8,0},{12,4},{16,24},{20,28},{24,16},{28,20},{1,9},{5... | collective-permute-start | bytes 98312 | tf_op jit(solution)/shard_map/ppermute | solution.py:450
  13.8 0.4 %collective-permute-start.3 = (f32[64,128]{1,0:T(8,128)S(1)}, f32[64,128]{1,0:T(8,128)S(1)}, u32[]{:S(2)}, u32[]{:S(2)}) collective-permute-start(f32[64,128]{1,0:T(8,128)S(1)} %get-tuple-element.51), channel_id=1, source_target_pairs={{0,12},{4,8},{8,4},{12,0},{16,28},{20,24},{24,20},{28,16},{1,13},{... | collective-permute-start | bytes 98312 | tf_op jit(solution)/shard_map/ppermute | solution.py:450
  14.1 0.4 %collective-permute-done.5 = f32[64,128]{1,0:T(8,128)S(1)} collective-permute-done((f32[64,128]{1,0:T(8,128)S(1)}, f32[64,128]{1,0:T(8,128)S(1)}, u32[]{:S(2)}, u32[]{:S(2)}) %collective-permute-start.5) | collective-permute-done | bytes 32800 | tf_op jit(solution)/shard_map/ppermute | solution.py:450
  14.6 1.5 %collective-permute-done.4 = f32[64,128]{1,0:T(8,128)S(1)} collective-permute-done((f32[64,128]{1,0:T(8,128)S(1)}, f32[64,128]{1,0:T(8,128)S(1)}, u32[]{:S(2)}, u32[]{:S(2)}) %collective-permute-start.4) | collective-permute-done | bytes 32800 | tf_op jit(solution)/shard_map/ppermute | solution.py:450
  16.1 2.5 %collective-permute-done.3 = f32[64,128]{1,0:T(8,128)S(1)} collective-permute-done((f32[64,128]{1,0:T(8,128)S(1)}, f32[64,128]{1,0:T(8,128)S(1)}, u32[]{:S(2)}, u32[]{:S(2)}) %collective-permute-start.3) | collective-permute-done | bytes 32800 | tf_op jit(solution)/shard_map/ppermute | solution.py:450
  18.6 0.5 %shard_map.94 = (f32[6,16,128]{2,1,0:T(8,128)S(1)}, f32[8,128]{1,0:T(8,128)S(1)}) custom-call(f32[48,128]{1,0:T(8,128)S(1)} %get-tuple-element.35.ring_a, f32[48,128]{1,0:T(8,128)S(1)} %get-tuple-element.34.ring_b, f32[8,8,128]{2,1,0:T(8,128)S(1)} %bitcast.40, f32[6,16,128]{2,1,0:T(8,128)S(1)} %get-tuple-element.18.flow, ...), custom_call_target="tpu_custom_call" | custom-call | tf_op jit(solution)/shard_map/pallas_call | solution.py:572
  19.1 2.1 %collective-permute-start.6 = (f32[40,128]{1,0:T(8,128)S(1)}, f32[40,128]{1,0:T(8,128)S(1)}, u32[]{:S(2)}, u32[]{:S(2)}) collective-permute-start(f32[40,128]{1,0:T(8,128)S(1)} %pad_maximum_fusion.7), channel_id=1, source_target_pairs={{0,16},{4,20},{8,24},{12,28},{16,0},{20,4},{24,8},{28,12},{1,17},{... | collective-permute-start | bytes 61448 | tf_op jit(solution)/shard_map/ppermute | solution.py:450
  21.1 0.6 %shard_map.96.sweep = f32[6,16,128]{2,1,0:T(8,128)S(1)} custom-call(f32[6,16,128]{2,1,0:T(8,128)S(1)} %get-tuple-element.30.residual, f32[36,16,128]{2,1,0:T(8,128)S(1)} %get-tuple-element.25.gain, f32[6,16,128]{2,1,0:T(8,128)S(1)} %get-tuple-element.26.source, f32[288,16,128]{2,1,0:T(8,128)S(1)} %get-tuple-element.24.scan), custom_call_target="tpu_custom_call" | custom-call | flops 1048576 | bytes 2097152 | tf_op jit(solution)/shard_map/pallas_call | solution.py:578
  21.7 2.1 %collective-permute-done.6 = f32[40,128]{1,0:T(8,128)S(1)} collective-permute-done((f32[40,128]{1,0:T(8,128)S(1)}, f32[40,128]{1,0:T(8,128)S(1)}, u32[]{:S(2)}, u32[]{:S(2)}) %collective-permute-start.6) | collective-permute-done | bytes 20512 | tf_op jit(solution)/shard_map/ppermute | solution.py:450
  23.9 0.5 %collective-permute-start.7 = (f32[8,128]{1,0:T(8,128)S(1)}, f32[8,128]{1,0:T(8,128)S(1)}, u32[]{:S(2)}, u32[]{:S(2)}) collective-permute-start(f32[8,128]{1,0:T(8,128)S(1)} %slice_add_fusion), channel_id=1, source_target_pairs={{0,4},{4,0},{8,12},{12,8},{16,20},{20,16},{24,28},{28,24},{1,5},{5... | collective-permute-start | bytes 12296 | tf_op jit(solution)/shard_map/ppermute | solution.py:450
  24.4 0.3 %collective-permute-start.8 = (f32[8,128]{1,0:T(8,128)S(1)}, f32[8,128]{1,0:T(8,128)S(1)}, u32[]{:S(2)}, u32[]{:S(2)}) collective-permute-start(f32[8,128]{1,0:T(8,128)S(1)} %slice_add_fusion), channel_id=1, source_target_pairs={{0,8},{4,12},{8,0},{12,4},{16,24},{20,28},{24,16},{28,20},{1,9},{5... | collective-permute-start | bytes 12296 | tf_op jit(solution)/shard_map/ppermute | solution.py:450
  24.7 2.6 %collective-permute-start.9 = (f32[8,128]{1,0:T(8,128)S(1)}, f32[8,128]{1,0:T(8,128)S(1)}, u32[]{:S(2)}, u32[]{:S(2)}) collective-permute-start(f32[8,128]{1,0:T(8,128)S(1)} %slice_add_fusion), channel_id=1, source_target_pairs={{0,12},{4,8},{8,4},{12,0},{16,28},{20,24},{24,20},{28,16},{1,13},{... | collective-permute-start | bytes 12296 | tf_op jit(solution)/shard_map/ppermute | solution.py:450
  27.4 0.9 %shard_map.95.weights = f32[48,128]{1,0:T(8,128)S(1)} custom-call(f32[8,8,128]{2,1,0:T(8,128)S(1)} %pad_maximum_fusion.6.ring), custom_call_target="tpu_custom_call" | custom-call | tf_op jit(solution)/shard_map/pallas_call | solution.py:588
  28.3 0.0 collective-permute-done.7
  28.3 0.0 collective-permute-done.8
  28.3 0.9 %collective-permute-done.9 = f32[8,128]{1,0:T(8,128)S(1)} collective-permute-done((f32[8,128]{1,0:T(8,128)S(1)}, f32[8,128]{1,0:T(8,128)S(1)}, u32[]{:S(2)}, u32[]{:S(2)}) %collective-permute-start.9) | collective-permute-done | bytes 4128 | tf_op jit(solution)/shard_map/ppermute | solution.py:450
  29.2 0.7 %shard_map.97 = f32[6,16,128]{2,1,0:T(8,128)} custom-call(f32[8,128]{1,0:T(8,128)S(1)} %add_add_fusion.gathered, f32[48,128]{1,0:T(8,128)S(1)} %shard_map.95.weights, f32[6,16,128]{2,1,0:T(8,128)S(1)} %get-tuple-element.18.flow, f32[288,16,128]{2,1,0:T(8,128)S(1)} %get-tuple-element.24.scan, f32[6,16,128]{2,1,0:T(8,128)S(1)} %shard_map.96.sweep), custom_call_target="tpu_custom_call" | custom-call | tf_op jit(solution)/shard_map/pallas_call | solution.py:597
  (16 shorter events, 0.1 us)
Async XLA Ops:
  0.9 9.1 %collective-permute-start = (f32[48,128]{1,0:T(8,128)S(1)}, f32[48,128]{1,0:T(8,128)S(1)}, u32[]{:S(2)}, u32[]{:S(2)}) collective-permute-start(f32[48,128]{1,0:T(8,128)S(1)} %get-tuple-element.21), channel_id=1, source_target_pairs={{0,17},{1,18},{2,19},{3,16},{4,21},{5,22},{6,23},{7,20},{8,25},{9,... | collective-permute-start | bytes 73736 | tf_op jit(solution)/shard_map/ppermute | solution.py:454
  4.5 5.5 %collective-permute-start.1 = (f32[48,128]{1,0:T(8,128)S(1)}, f32[48,128]{1,0:T(8,128)S(1)}, u32[]{:S(2)}, u32[]{:S(2)}) collective-permute-start(f32[48,128]{1,0:T(8,128)S(1)} %get-tuple-element.21), channel_id=1, source_target_pairs={{0,1},{1,2},{2,3},{3,0},{4,5},{5,6},{6,7},{7,4},{8,9},{9,10},{10,1... | collective-permute-start | bytes 73736 | tf_op jit(solution)/shard_map/ppermute | solution.py:454
  6.1 4.5 %collective-permute-start.2 = (f32[8,128]{1,0:T(8,128)S(1)}, f32[8,128]{1,0:T(8,128)S(1)}, u32[]{:S(2)}, u32[]{:S(2)}) collective-permute-start(f32[8,128]{1,0:T(8,128)S(1)} %get-tuple-element.19.halo), channel_id=1, source_target_pairs={{0,16},{4,20},{8,24},{12,28},{16,0},{20,4},{24,8},{28,12},{1,17},{... | collective-permute-start | bytes 12296 | tf_op jit(solution)/shard_map/ppermute | solution.py:450
  10.6 4.0 %collective-permute-start.5 = (f32[64,128]{1,0:T(8,128)S(1)}, f32[64,128]{1,0:T(8,128)S(1)}, u32[]{:S(2)}, u32[]{:S(2)}) collective-permute-start(f32[64,128]{1,0:T(8,128)S(1)} %get-tuple-element.53), channel_id=1, source_target_pairs={{0,4},{4,0},{8,12},{12,8},{16,20},{20,16},{24,28},{28,24},{1,5},{5... | collective-permute-start | bytes 98312 | tf_op jit(solution)/shard_map/ppermute | solution.py:450
  12.2 3.9 %collective-permute-start.4 = (f32[64,128]{1,0:T(8,128)S(1)}, f32[64,128]{1,0:T(8,128)S(1)}, u32[]{:S(2)}, u32[]{:S(2)}) collective-permute-start(f32[64,128]{1,0:T(8,128)S(1)} %get-tuple-element.52), channel_id=1, source_target_pairs={{0,8},{4,12},{8,0},{12,4},{16,24},{20,28},{24,16},{28,20},{1,9},{5... | collective-permute-start | bytes 98312 | tf_op jit(solution)/shard_map/ppermute | solution.py:450
  13.8 4.8 %collective-permute-start.3 = (f32[64,128]{1,0:T(8,128)S(1)}, f32[64,128]{1,0:T(8,128)S(1)}, u32[]{:S(2)}, u32[]{:S(2)}) collective-permute-start(f32[64,128]{1,0:T(8,128)S(1)} %get-tuple-element.51), channel_id=1, source_target_pairs={{0,12},{4,8},{8,4},{12,0},{16,28},{20,24},{24,20},{28,16},{1,13},{... | collective-permute-start | bytes 98312 | tf_op jit(solution)/shard_map/ppermute | solution.py:450
  19.1 4.8 %collective-permute-start.6 = (f32[40,128]{1,0:T(8,128)S(1)}, f32[40,128]{1,0:T(8,128)S(1)}, u32[]{:S(2)}, u32[]{:S(2)}) collective-permute-start(f32[40,128]{1,0:T(8,128)S(1)} %pad_maximum_fusion.7), channel_id=1, source_target_pairs={{0,16},{4,20},{8,24},{12,28},{16,0},{20,4},{24,8},{28,12},{1,17},{... | collective-permute-start | bytes 61448 | tf_op jit(solution)/shard_map/ppermute | solution.py:450
  23.9 4.4 %collective-permute-start.7 = (f32[8,128]{1,0:T(8,128)S(1)}, f32[8,128]{1,0:T(8,128)S(1)}, u32[]{:S(2)}, u32[]{:S(2)}) collective-permute-start(f32[8,128]{1,0:T(8,128)S(1)} %slice_add_fusion), channel_id=1, source_target_pairs={{0,4},{4,0},{8,12},{12,8},{16,20},{20,16},{24,28},{28,24},{1,5},{5... | collective-permute-start | bytes 12296 | tf_op jit(solution)/shard_map/ppermute | solution.py:450
  24.4 3.9 %collective-permute-start.8 = (f32[8,128]{1,0:T(8,128)S(1)}, f32[8,128]{1,0:T(8,128)S(1)}, u32[]{:S(2)}, u32[]{:S(2)}) collective-permute-start(f32[8,128]{1,0:T(8,128)S(1)} %slice_add_fusion), channel_id=1, source_target_pairs={{0,8},{4,12},{8,0},{12,4},{16,24},{20,28},{24,16},{28,20},{1,9},{5... | collective-permute-start | bytes 12296 | tf_op jit(solution)/shard_map/ppermute | solution.py:450
  24.7 4.5 %collective-permute-start.9 = (f32[8,128]{1,0:T(8,128)S(1)}, f32[8,128]{1,0:T(8,128)S(1)}, u32[]{:S(2)}, u32[]{:S(2)}) collective-permute-start(f32[8,128]{1,0:T(8,128)S(1)} %slice_add_fusion), channel_id=1, source_target_pairs={{0,12},{4,8},{8,4},{12,0},{16,28},{20,24},{24,20},{28,16},{1,13},{... | collective-permute-start | bytes 12296 | tf_op jit(solution)/shard_map/ppermute | solution.py:450

commit v3 on v2

--- a/solution.py
+++ b/solution.py
@@ -580,11 +580,11 @@
         out_shape=shape(FIELDS, lines, cells),
         in_specs=[VMEM] * 4,
         out_specs=VMEM,
-        cost_estimate=pl.CostEstimate(flops=1 << 20, bytes_accessed=1 << 21, transcendentals=0),
     )(residual, gain, source, scan)
-    values = exchange(jnp.concatenate([ends, ring[:, 0].reshape(top * HALF, cells)], axis=0), sectors, top)
-    ends = ends + values[:end_rows]
-    maps = jnp.concatenate([ring[:, 0], values[end_rows:].reshape(top, HALF, cells)], axis=0)
+    across = exchange(ends, sectors, top)
+    others = exchange(ring[:, 0].reshape(top * HALF, cells), sectors, top)
+    ends = ends + across
+    maps = jnp.concatenate([ring[:, 0], others.reshape(top, HALF, cells)], axis=0)
     weights = call(
         functools.partial(closing_kernel, sectors),
         out_shape=shape(FIELDS * end_rows, cells),
@@ -592,7 +592,10 @@
         out_specs=VMEM,
     )(maps)
     for masks in groups(sectors):
-        for values in [exchange(ends, sectors, mask) for mask in masks]:
+        arrived = []
+        for mask in masks:
+            arrived.append(exchange(ends, sectors, mask))
+        for values in arrived:
             ends = ends + values
     new_state = call(
         functools.partial(finish_kernel, sectors, levels),

time: 30.1 us -> 34.3 us (1.14)
  starting transfers between devices: 14.6 us -> 16.7 us
  waiting for transfers between devices: 8.02 us -> 10.1 us
    ppermute x8 -> x9, starting transfers between devices: 9.44 us -> 11.6 us  [exchange(): return lax.ppermute(values, 'azim', [(i, i ^ mask) for i in range(sectors)])]
    ppermute x8 -> x9, waiting for transfers between devices: 8.02 us -> 10 us  [exchange(): return lax.ppermute(values, 'azim', [(i, i ^ mask) for i in range(sectors)])]
  transfers between devices with their start and end apart: 10 -> 11, of which waited for: 6 -> 6; matrix products, arithmetic and copies ran while one was open for 0% -> 0% of each run, Pallas kernels for 17% -> 12%
where the time goes in v3:
time: 34.3 us; the launch traced here: 34.1 us
  starting transfers between devices  16.7 us (49%)
  waiting for transfers between devices  10.1 us (29%)
  Pallas kernels  7.14 us (21%)
    ppermute x9, starting transfers between devices, exchange(): return lax.ppermute(values, 'azim', [(i, i ^ mask) for i in range(sectors)])  11.6 us
    ppermute x9, waiting for transfers between devices, exchange(): return lax.ppermute(values, 'azim', [(i, i ^ mask) for i in range(sectors)])  10 us
    ppermute x2, starting transfers between devices, from_upstream(): lax.ppermute(values, ('azim', 'row'), [(i * row_count + r, (i ^ mask) * r...  5.16 us
    pallas_call x1, Pallas kernels, shards(): call(functools.partial(prepare_kernel, sectors, levels), out_shape=(shape...  2.41 us
    pallas_call x1, Pallas kernels, shards(): call(functools.partial(reach_kernel, sectors, levels), out_shape=(shape(3...  1.12 us
    pallas_call x1, Pallas kernels, shards(): call(functools.partial(closing_kernel, sectors), out_shape=shape(FIELDS *...  0.93 us
    pallas_call x1, Pallas kernels, shards(): call(edges_kernel, out_shape=(shape(FIELDS, lines, cells), shape(count, c...  0.9 us
    pallas_call x1, Pallas kernels, shards(): call(functools.partial(finish_kernel, sectors, levels), out_shape=shape(F...  0.73 us
  transfers between devices with their start and end apart: 11, of which 6 were waited for; matrix products, arithmetic and copies ran while one was open for 0% of the time, Pallas kernels for 12%

profile of v3, /device:TPU:0, one launch (start us, length us, event | category | flops | bytes accessed | tf_op | source)
XLA Modules:
  0.0 34.1 jit_solution(9753925612513116902)
XLA Ops:
  0.0 0.9 %shard_map.91 = (f32[6,16,128]{2,1,0:T(8,128)S(1)}, f32[48,128]{1,0:T(8,128)S(1)}, f32[8,128]{1,0:T(8,128)S(1)}) custom-call(f32[6,16,128]{2,1,0:T(8,128)} %bitcast.42), custom_call_target="tpu_custom_call" | custom-call | tf_op jit(solution)/shard_map/pallas_call | solution.py:496
  0.9 3.6 %collective-permute-start = (f32[48,128]{1,0:T(8,128)S(1)}, f32[48,128]{1,0:T(8,128)S(1)}, u32[]{:S(2)}, u32[]{:S(2)}) collective-permute-start(f32[48,128]{1,0:T(8,128)S(1)} %get-tuple-element.21), channel_id=1, source_target_pairs={{0,17},{1,18},{2,19},{3,16},{4,21},{5,22},{6,23},{7,20},{8,25},{9,... | collective-permute-start | bytes 73736 | tf_op jit(solution)/shard_map/ppermute | solution.py:454
  4.5 1.6 %collective-permute-start.1 = (f32[48,128]{1,0:T(8,128)S(1)}, f32[48,128]{1,0:T(8,128)S(1)}, u32[]{:S(2)}, u32[]{:S(2)}) collective-permute-start(f32[48,128]{1,0:T(8,128)S(1)} %get-tuple-element.21), channel_id=1, source_target_pairs={{0,1},{1,2},{2,3},{3,0},{4,5},{5,6},{6,7},{7,4},{8,9},{9,10},{10,1... | collective-permute-start | bytes 73736 | tf_op jit(solution)/shard_map/ppermute | solution.py:454
  6.1 0.3 collective-permute-start.2
  6.4 2.4 %shard_map.92 = (f32[36,16,128]{2,1,0:T(8,128)S(1)}, f32[6,16,128]{2,1,0:T(8,128)S(1)}, f32[80,128]{1,0:T(8,128)S(1)}, s32[16,128]{1,0:T(8,128)S(1)}, f32[8,128]{1,0:T(8,128)S(1)}, /*index=5*/f32[288,16,128]{2,1,0:T(8,128)S(1)}) custom-call(f32[6,16,128]{2,1,0:T(8,128)S(1)} %get-tuple-element.18.flow, f32[8,128]{1,0:T(8,128)S(1)} %get-tuple-element.19.halo, ...), custom_call_target="tpu_custom_call" | custom-call | tf_op jit(solution)/shard_map/pallas_call | solution.py:507
  8.9 1.1 %shard_map.93 = (f32[36,16,128]{2,1,0:T(8,128)S(1)}, f32[8,128]{1,0:T(8,128)S(1)}) custom-call(f32[288,16,128]{2,1,0:T(8,128)S(1)} %get-tuple-element.24.scan, f32[36,16,128]{2,1,0:T(8,128)S(1)} %get-tuple-element.25.gain, f32[6,16,128]{2,1,0:T(8,128)S(1)} %get-tuple-element.26.source), custom_call_target="tpu_custom_call" | custom-call | tf_op jit(solution)/shard_map/pallas_call | solution.py:565
  10.0 0.0 collective-permute-done
  10.0 0.0 collective-permute-done.1
  10.0 0.6 %collective-permute-done.2 = f32[8,128]{1,0:T(8,128)S(1)} collective-permute-done((f32[8,128]{1,0:T(8,128)S(1)}, f32[8,128]{1,0:T(8,128)S(1)}, u32[]{:S(2)}, u32[]{:S(2)}) %collective-permute-start.2) | collective-permute-done | bytes 4128 | tf_op jit(solution)/shard_map/ppermute | solution.py:450
  10.6 1.6 %collective-permute-start.5 = (f32[64,128]{1,0:T(8,128)S(1)}, f32[64,128]{1,0:T(8,128)S(1)}, u32[]{:S(2)}, u32[]{:S(2)}) collective-permute-start(f32[64,128]{1,0:T(8,128)S(1)} %get-tuple-element.53), channel_id=1, source_target_pairs={{0,4},{4,0},{8,12},{12,8},{16,20},{20,16},{24,28},{28,24},{1,5},{5... | collective-permute-start | bytes 98312 | tf_op jit(solution)/shard_map/ppermute | solution.py:450
  12.2 1.6 %collective-permute-start.4 = (f32[64,128]{1,0:T(8,128)S(1)}, f32[64,128]{1,0:T(8,128)S(1)}, u32[]{:S(2)}, u32[]{:S(2)}) collective-permute-start(f32[64,128]{1,0:T(8,128)S(1)} %get-tuple-element.52), channel_id=1, source_target_pairs={{0,8},{4,12},{8,0},{12,4},{16,24},{20,28},{24,16},{28,20},{1,9},{5... | collective-permute-start | bytes 98312 | tf_op jit(solution)/shard_map/ppermute | solution.py:450
  13.8 0.4 %collective-permute-start.3 = (f32[64,128]{1,0:T(8,128)S(1)}, f32[64,128]{1,0:T(8,128)S(1)}, u32[]{:S(2)}, u32[]{:S(2)}) collective-permute-start(f32[64,128]{1,0:T(8,128)S(1)} %get-tuple-element.51), channel_id=1, source_target_pairs={{0,12},{4,8},{8,4},{12,0},{16,28},{20,24},{24,20},{28,16},{1,13},{... | collective-permute-start | bytes 98312 | tf_op jit(solution)/shard_map/ppermute | solution.py:450
  14.1 0.4 %collective-permute-done.5 = f32[64,128]{1,0:T(8,128)S(1)} collective-permute-done((f32[64,128]{1,0:T(8,128)S(1)}, f32[64,128]{1,0:T(8,128)S(1)}, u32[]{:S(2)}, u32[]{:S(2)}) %collective-permute-start.5) | collective-permute-done | bytes 32800 | tf_op jit(solution)/shard_map/ppermute | solution.py:450
  14.6 1.5 %collective-permute-done.4 = f32[64,128]{1,0:T(8,128)S(1)} collective-permute-done((f32[64,128]{1,0:T(8,128)S(1)}, f32[64,128]{1,0:T(8,128)S(1)}, u32[]{:S(2)}, u32[]{:S(2)}) %collective-permute-start.4) | collective-permute-done | bytes 32800 | tf_op jit(solution)/shard_map/ppermute | solution.py:450
  16.1 2.5 %collective-permute-done.3 = f32[64,128]{1,0:T(8,128)S(1)} collective-permute-done((f32[64,128]{1,0:T(8,128)S(1)}, f32[64,128]{1,0:T(8,128)S(1)}, u32[]{:S(2)}, u32[]{:S(2)}) %collective-permute-start.3) | collective-permute-done | bytes 32800 | tf_op jit(solution)/shard_map/ppermute | solution.py:450
  18.6 0.5 %shard_map.94 = (f32[6,16,128]{2,1,0:T(8,128)S(1)}, f32[8,128]{1,0:T(8,128)S(1)}) custom-call(f32[48,128]{1,0:T(8,128)S(1)} %get-tuple-element.35.ring_a, f32[48,128]{1,0:T(8,128)S(1)} %get-tuple-element.34.ring_b, f32[8,8,128]{2,1,0:T(8,128)S(1)} %bitcast.38, f32[6,16,128]{2,1,0:T(8,128)S(1)} %get-tuple-element.18.flow, ...), custom_call_target="tpu_custom_call" | custom-call | tf_op jit(solution)/shard_map/pallas_call | solution.py:572
  19.0 2.1 %collective-permute-start.6 = (f32[8,128]{1,0:T(8,128)S(1)}, f32[8,128]{1,0:T(8,128)S(1)}, u32[]{:S(2)}, u32[]{:S(2)}) collective-permute-start(f32[8,128]{1,0:T(8,128)S(1)} %get-tuple-element.29), channel_id=1, source_target_pairs={{0,16},{4,20},{8,24},{12,28},{16,0},{20,4},{24,8},{28,12},{1,17},{... | collective-permute-start | bytes 12296 | tf_op jit(solution)/shard_map/ppermute | solution.py:450
  21.1 2.5 %collective-permute-done.6 = f32[8,128]{1,0:T(8,128)S(1)} collective-permute-done((f32[8,128]{1,0:T(8,128)S(1)}, f32[8,128]{1,0:T(8,128)S(1)}, u32[]{:S(2)}, u32[]{:S(2)}) %collective-permute-start.6) | collective-permute-done | bytes 4128 | tf_op jit(solution)/shard_map/ppermute | solution.py:450
  23.6 0.5 %collective-permute-start.7 = (f32[8,128]{1,0:T(8,128)S(1)}, f32[8,128]{1,0:T(8,128)S(1)}, u32[]{:S(2)}, u32[]{:S(2)}) collective-permute-start(f32[8,128]{1,0:T(8,128)S(1)} %add.12), channel_id=1, source_target_pairs={{0,4},{4,0},{8,12},{12,8},{16,20},{20,16},{24,28},{28,24},{1,5},{5... | collective-permute-start | bytes 12296 | tf_op jit(solution)/shard_map/ppermute | solution.py:450
  24.1 0.4 %collective-permute-start.8 = (f32[8,128]{1,0:T(8,128)S(1)}, f32[8,128]{1,0:T(8,128)S(1)}, u32[]{:S(2)}, u32[]{:S(2)}) collective-permute-start(f32[8,128]{1,0:T(8,128)S(1)} %add.12), channel_id=1, source_target_pairs={{0,8},{4,12},{8,0},{12,4},{16,24},{20,28},{24,16},{28,20},{1,9},{5... | collective-permute-start | bytes 12296 | tf_op jit(solution)/shard_map/ppermute | solution.py:450
  24.5 2.5 %collective-permute-start.9 = (f32[8,128]{1,0:T(8,128)S(1)}, f32[8,128]{1,0:T(8,128)S(1)}, u32[]{:S(2)}, u32[]{:S(2)}) collective-permute-start(f32[8,128]{1,0:T(8,128)S(1)} %add.12), channel_id=1, source_target_pairs={{0,12},{4,8},{8,4},{12,0},{16,28},{20,24},{24,20},{28,16},{1,13},{... | collective-permute-start | bytes 12296 | tf_op jit(solution)/shard_map/ppermute | solution.py:450
  27.1 0.6 %shard_map.96.sweep = f32[6,16,128]{2,1,0:T(8,128)S(1)} custom-call(f32[6,16,128]{2,1,0:T(8,128)S(1)} %get-tuple-element.30.residual, f32[36,16,128]{2,1,0:T(8,128)S(1)} %get-tuple-element.25.gain, f32[6,16,128]{2,1,0:T(8,128)S(1)} %get-tuple-element.26.source, f32[288,16,128]{2,1,0:T(8,128)S(1)} %get-tuple-element.24.scan), custom_call_target="tpu_custom_call" | custom-call | tf_op jit(solution)/shard_map/pallas_call | solution.py:578
  27.7 2.1 %collective-permute-start.10 = (f32[32,128]{1,0:T(8,128)S(1)}, f32[32,128]{1,0:T(8,128)S(1)}, u32[]{:S(2)}, u32[]{:S(2)}) collective-permute-start(f32[32,128]{1,0:T(8,128)S(1)} %get-tuple-element.39), channel_id=1, source_target_pairs={{0,16},{4,20},{8,24},{12,28},{16,0},{20,4},{24,8},{28,12},{1,17},{... | collective-permute-start | bytes 49160 | tf_op jit(solution)/shard_map/ppermute | solution.py:450
  29.8 0.0 collective-permute-done.7
  29.8 0.0 collective-permute-done.8
  29.8 0.0 collective-permute-done.9
  29.8 2.6 %collective-permute-done.10 = f32[32,128]{1,0:T(8,128)S(1)} collective-permute-done((f32[32,128]{1,0:T(8,128)S(1)}, f32[32,128]{1,0:T(8,128)S(1)}, u32[]{:S(2)}, u32[]{:S(2)}) %collective-permute-start.10) | collective-permute-done | bytes 16416 | tf_op jit(solution)/shard_map/ppermute | solution.py:450
  32.4 0.9 %shard_map.95.weights = f32[48,128]{1,0:T(8,128)S(1)} custom-call(f32[8,8,128]{2,1,0:T(8,128)S(1)} %pad_maximum_fusion.6.ring), custom_call_target="tpu_custom_call" | custom-call | tf_op jit(solution)/shard_map/pallas_call | solution.py:588
  33.4 0.7 %shard_map.97 = f32[6,16,128]{2,1,0:T(8,128)} custom-call(f32[8,128]{1,0:T(8,128)S(1)} %add_add_fusion.gathered, f32[48,128]{1,0:T(8,128)S(1)} %shard_map.95.weights, f32[6,16,128]{2,1,0:T(8,128)S(1)} %get-tuple-element.18.flow, f32[288,16,128]{2,1,0:T(8,128)S(1)} %get-tuple-element.24.scan, f32[6,16,128]{2,1,0:T(8,128)S(1)} %shard_map.96.sweep), custom_call_target="tpu_custom_call" | custom-call | tf_op jit(solution)/shard_map/pallas_call | solution.py:600
  (14 shorter events, 0.1 us)
Async XLA Ops:
  0.9 9.1 %collective-permute-start = (f32[48,128]{1,0:T(8,128)S(1)}, f32[48,128]{1,0:T(8,128)S(1)}, u32[]{:S(2)}, u32[]{:S(2)}) collective-permute-start(f32[48,128]{1,0:T(8,128)S(1)} %get-tuple-element.21), channel_id=1, source_target_pairs={{0,17},{1,18},{2,19},{3,16},{4,21},{5,22},{6,23},{7,20},{8,25},{9,... | collective-permute-start | bytes 73736 | tf_op jit(solution)/shard_map/ppermute | solution.py:454
  4.5 5.5 %collective-permute-start.1 = (f32[48,128]{1,0:T(8,128)S(1)}, f32[48,128]{1,0:T(8,128)S(1)}, u32[]{:S(2)}, u32[]{:S(2)}) collective-permute-start(f32[48,128]{1,0:T(8,128)S(1)} %get-tuple-element.21), channel_id=1, source_target_pairs={{0,1},{1,2},{2,3},{3,0},{4,5},{5,6},{6,7},{7,4},{8,9},{9,10},{10,1... | collective-permute-start | bytes 73736 | tf_op jit(solution)/shard_map/ppermute | solution.py:454
  6.1 4.5 %collective-permute-start.2 = (f32[8,128]{1,0:T(8,128)S(1)}, f32[8,128]{1,0:T(8,128)S(1)}, u32[]{:S(2)}, u32[]{:S(2)}) collective-permute-start(f32[8,128]{1,0:T(8,128)S(1)} %get-tuple-element.19.halo), channel_id=1, source_target_pairs={{0,16},{4,20},{8,24},{12,28},{16,0},{20,4},{24,8},{28,12},{1,17},{... | collective-permute-start | bytes 12296 | tf_op jit(solution)/shard_map/ppermute | solution.py:450
  10.6 4.0 %collective-permute-start.5 = (f32[64,128]{1,0:T(8,128)S(1)}, f32[64,128]{1,0:T(8,128)S(1)}, u32[]{:S(2)}, u32[]{:S(2)}) collective-permute-start(f32[64,128]{1,0:T(8,128)S(1)} %get-tuple-element.53), channel_id=1, source_target_pairs={{0,4},{4,0},{8,12},{12,8},{16,20},{20,16},{24,28},{28,24},{1,5},{5... | collective-permute-start | bytes 98312 | tf_op jit(solution)/shard_map/ppermute | solution.py:450
  12.2 3.9 %collective-permute-start.4 = (f32[64,128]{1,0:T(8,128)S(1)}, f32[64,128]{1,0:T(8,128)S(1)}, u32[]{:S(2)}, u32[]{:S(2)}) collective-permute-start(f32[64,128]{1,0:T(8,128)S(1)} %get-tuple-element.52), channel_id=1, source_target_pairs={{0,8},{4,12},{8,0},{12,4},{16,24},{20,28},{24,16},{28,20},{1,9},{5... | collective-permute-start | bytes 98312 | tf_op jit(solution)/shard_map/ppermute | solution.py:450
  13.8 4.8 %collective-permute-start.3 = (f32[64,128]{1,0:T(8,128)S(1)}, f32[64,128]{1,0:T(8,128)S(1)}, u32[]{:S(2)}, u32[]{:S(2)}) collective-permute-start(f32[64,128]{1,0:T(8,128)S(1)} %get-tuple-element.51), channel_id=1, source_target_pairs={{0,12},{4,8},{8,4},{12,0},{16,28},{20,24},{24,20},{28,16},{1,13},{... | collective-permute-start | bytes 98312 | tf_op jit(solution)/shard_map/ppermute | solution.py:450
  19.0 4.5 %collective-permute-start.6 = (f32[8,128]{1,0:T(8,128)S(1)}, f32[8,128]{1,0:T(8,128)S(1)}, u32[]{:S(2)}, u32[]{:S(2)}) collective-permute-start(f32[8,128]{1,0:T(8,128)S(1)} %get-tuple-element.29), channel_id=1, source_target_pairs={{0,16},{4,20},{8,24},{12,28},{16,0},{20,4},{24,8},{28,12},{1,17},{... | collective-permute-start | bytes 12296 | tf_op jit(solution)/shard_map/ppermute | solution.py:450
  23.6 6.2 %collective-permute-start.7 = (f32[8,128]{1,0:T(8,128)S(1)}, f32[8,128]{1,0:T(8,128)S(1)}, u32[]{:S(2)}, u32[]{:S(2)}) collective-permute-start(f32[8,128]{1,0:T(8,128)S(1)} %add.12), channel_id=1, source_target_pairs={{0,4},{4,0},{8,12},{12,8},{16,20},{20,16},{24,28},{28,24},{1,5},{5... | collective-permute-start | bytes 12296 | tf_op jit(solution)/shard_map/ppermute | solution.py:450
  24.1 5.7 %collective-permute-start.8 = (f32[8,128]{1,0:T(8,128)S(1)}, f32[8,128]{1,0:T(8,128)S(1)}, u32[]{:S(2)}, u32[]{:S(2)}) collective-permute-start(f32[8,128]{1,0:T(8,128)S(1)} %add.12), channel_id=1, source_target_pairs={{0,8},{4,12},{8,0},{12,4},{16,24},{20,28},{24,16},{28,20},{1,9},{5... | collective-permute-start | bytes 12296 | tf_op jit(solution)/shard_map/ppermute | solution.py:450
  24.5 5.3 %collective-permute-start.9 = (f32[8,128]{1,0:T(8,128)S(1)}, f32[8,128]{1,0:T(8,128)S(1)}, u32[]{:S(2)}, u32[]{:S(2)}) collective-permute-start(f32[8,128]{1,0:T(8,128)S(1)} %add.12), channel_id=1, source_target_pairs={{0,12},{4,8},{8,4},{12,0},{16,28},{20,24},{24,20},{28,16},{1,13},{... | collective-permute-start | bytes 12296 | tf_op jit(solution)/shard_map/ppermute | solution.py:450
  27.7 4.8 %collective-permute-start.10 = (f32[32,128]{1,0:T(8,128)S(1)}, f32[32,128]{1,0:T(8,128)S(1)}, u32[]{:S(2)}, u32[]{:S(2)}) collective-permute-start(f32[32,128]{1,0:T(8,128)S(1)} %get-tuple-element.39), channel_id=1, source_target_pairs={{0,16},{4,20},{8,24},{12,28},{16,0},{20,4},{24,8},{28,12},{1,17},{... | collective-permute-start | bytes 49160 | tf_op jit(solution)/shard_map/ppermute | solution.py:450

commit v4 on v2

--- a/solution.py
+++ b/solution.py
@@ -428,7 +428,7 @@
             weights[pl.ds(row, HALF), :] = jnp.where(crossed, behind, ahead)
 
 
-def finish_kernel(sectors, levels, gathered, weights, flow, scan, sweep, out):
+def finish_kernel(sectors, levels, gathered, weights, flow, scan, sweep, out, held, sems):
     lane = lane_ids()
     count = pl.cdiv(FIELDS, packing(sectors))
     begin = [[None] * FIELDS for _ in range(2)]
@@ -440,10 +440,15 @@
         for half in range(2):
             total = jnp.sum(jnp.where((lane & 1) == half, acc, 0.0), axis=1, keepdims=True)
             begin[half][f] = jnp.broadcast_to(total, (HALF, LANES))
+    copies = []
     for half in range(2):
         gained = matvec([scan[36 * levels + e, rows(half), :] for e in range(36)], begin[half])
         for f in range(FIELDS):
-            out[f, rows(half), :] = flow[f, rows(half), :] + (gained[f] + sweep[f, rows(half), :])
+            held[half, f] = flow[f, rows(half), :] + (gained[f] + sweep[f, rows(half), :])
+        copies.append(pltpu.make_async_copy(held.at[half], out.at[:, rows(half), :], sems.at[half]))
+        copies[-1].start()
+    for copy in copies:
+        copy.wait()
 
 
 def exchange(values, sectors, mask):
@@ -550,10 +555,18 @@
     at = 2
     for masks in groups(sectors):
         on_a, on_b, to_a = (flags[at + k : at + k + 1] for k in range(3))
+        near_packs = ring.reshape(-1, 2, HALF, cells)[:, 0]
         arrived = []
         for mask in masks:
-            sent = jnp.concatenate([jnp.where(to_a == mask, ring_a, ring_b), ring], axis=0)
-            arrived.append(exchange(sent, sectors, mask))
+            slim = mask in (1, 2)
+            packs = near_packs.reshape(-1, cells) if slim else ring
+            sent = jnp.concatenate([jnp.where(to_a == mask, ring_a, ring_b), packs], axis=0)
+            values = exchange(sent, sectors, mask)
+            if slim:
+                got = values[count:].reshape(near_packs.shape)
+                both = jnp.stack([got, jnp.zeros_like(got)], axis=1).reshape(-1, cells)
+                values = jnp.concatenate([values[:count], both], axis=0)
+            arrived.append(values)
         for mask, values in zip(masks, arrived):
             ring_a = jnp.where(on_a == mask, values[:count], ring_a)
             ring_b = jnp.where(on_b == mask, values[:count], ring_b)
@@ -598,7 +611,11 @@
         functools.partial(finish_kernel, sectors, levels),
         out_shape=shape(FIELDS, lines, cells),
         in_specs=[VMEM] * 5,
-        out_specs=VMEM,
+        out_specs=HBM,
+        scratch_shapes=[
+            pltpu.VMEM((2, FIELDS, HALF, cells), jnp.float32),
+            pltpu.SemaphoreType.DMA((2,)),
+        ],
     )(ends, weights, flow, scan, sweep)
     return new_state.reshape(flow_state.shape)
 

time: 30.1 us -> 30.2 us (level)
  no operation moved by 1% of the time
where the time goes in v4:
time: 30.2 us; the launch traced here: 30 us
  starting transfers between devices  14.6 us (48%)
  waiting for transfers between devices  8.09 us (27%)
  Pallas kernels  7.15 us (24%)
    ppermute x8, starting transfers between devices, exchange(): return lax.ppermute(values, 'azim', [(i, i ^ mask) for i in range(sectors)])  9.41 us
    ppermute x8, waiting for transfers between devices, exchange(): return lax.ppermute(values, 'azim', [(i, i ^ mask) for i in range(sectors)])  8.09 us
    ppermute x2, starting transfers between devices, from_upstream(): lax.ppermute(values, ('azim', 'row'), [(i * row_count + r, (i ^ mask) * r...  5.16 us
    pallas_call x1, Pallas kernels, shards(): call(functools.partial(prepare_kernel, sectors, levels), out_shape=(shape...  2.41 us
    pallas_call x1, Pallas kernels, shards(): call(functools.partial(reach_kernel, sectors, levels), out_shape=(shape(3...  1.12 us
    pallas_call x1, Pallas kernels, shards(): call(functools.partial(closing_kernel, sectors), out_shape=shape(FIELDS *...  0.93 us
    pallas_call x1, Pallas kernels, shards(): call(edges_kernel, out_shape=(shape(FIELDS, lines, cells), shape(count, c...  0.9 us
    pallas_call x1, Pallas kernels, shards(): call(functools.partial(finish_kernel, sectors, levels), out_shape=shape(F...  0.74 us
  transfers between devices with their start and end apart: 10, of which 6 were waited for; matrix products, arithmetic and copies ran while one was open for 0% of the time, Pallas kernels for 17%

profile of v4, /device:TPU:0, one launch (start us, length us, event | category | flops | bytes accessed | tf_op | source)
XLA Modules:
  0.0 30.0 jit_solution(1007697433795098570)
XLA Ops:
  0.0 0.9 %shard_map.91 = (f32[6,16,128]{2,1,0:T(8,128)S(1)}, f32[48,128]{1,0:T(8,128)S(1)}, f32[8,128]{1,0:T(8,128)S(1)}) custom-call(f32[6,16,128]{2,1,0:T(8,128)} %bitcast.55), custom_call_target="tpu_custom_call" | custom-call | tf_op jit(solution)/shard_map/pallas_call | solution.py:501
  0.9 3.6 %collective-permute-start = (f32[48,128]{1,0:T(8,128)S(1)}, f32[48,128]{1,0:T(8,128)S(1)}, u32[]{:S(2)}, u32[]{:S(2)}) collective-permute-start(f32[48,128]{1,0:T(8,128)S(1)} %get-tuple-element.21), channel_id=1, source_target_pairs={{0,17},{1,18},{2,19},{3,16},{4,21},{5,22},{6,23},{7,20},{8,25},{9,... | collective-permute-start | bytes 73736 | tf_op jit(solution)/shard_map/ppermute | solution.py:459
  4.5 1.6 %collective-permute-start.1 = (f32[48,128]{1,0:T(8,128)S(1)}, f32[48,128]{1,0:T(8,128)S(1)}, u32[]{:S(2)}, u32[]{:S(2)}) collective-permute-start(f32[48,128]{1,0:T(8,128)S(1)} %get-tuple-element.21), channel_id=1, source_target_pairs={{0,1},{1,2},{2,3},{3,0},{4,5},{5,6},{6,7},{7,4},{8,9},{9,10},{10,1... | collective-permute-start | bytes 73736 | tf_op jit(solution)/shard_map/ppermute | solution.py:459
  6.1 0.3 %collective-permute-start.2 = (f32[8,128]{1,0:T(8,128)S(1)}, f32[8,128]{1,0:T(8,128)S(1)}, u32[]{:S(2)}, u32[]{:S(2)}) collective-permute-start(f32[8,128]{1,0:T(8,128)S(1)} %get-tuple-element.19.halo), channel_id=1, source_target_pairs={{0,16},{4,20},{8,24},{12,28},{16,0},{20,4},{24,8},{28,12},{1,17},{... | collective-permute-start | bytes 12296 | tf_op jit(solution)/shard_map/ppermute | solution.py:455
  6.4 2.4 %shard_map.92 = (f32[36,16,128]{2,1,0:T(8,128)S(1)}, f32[6,16,128]{2,1,0:T(8,128)S(1)}, f32[80,128]{1,0:T(8,128)S(1)}, s32[16,128]{1,0:T(8,128)S(1)}, f32[8,128]{1,0:T(8,128)S(1)}, /*index=5*/f32[288,16,128]{2,1,0:T(8,128)S(1)}) custom-call(f32[6,16,128]{2,1,0:T(8,128)S(1)} %get-tuple-element.18.flow, f32[8,128]{1,0:T(8,128)S(1)} %get-tuple-element.19.halo, ...), custom_call_target="tpu_custom_call" | custom-call | tf_op jit(solution)/shard_map/pallas_call | solution.py:512
  8.9 1.1 %shard_map.93 = (f32[36,16,128]{2,1,0:T(8,128)S(1)}, f32[8,128]{1,0:T(8,128)S(1)}) custom-call(f32[288,16,128]{2,1,0:T(8,128)S(1)} %get-tuple-element.24.scan, f32[36,16,128]{2,1,0:T(8,128)S(1)} %get-tuple-element.25.gain, f32[6,16,128]{2,1,0:T(8,128)S(1)} %get-tuple-element.26.source), custom_call_target="tpu_custom_call" | custom-call | tf_op jit(solution)/shard_map/pallas_call | solution.py:578
  10.0 0.6 %collective-permute-done.2 = f32[8,128]{1,0:T(8,128)S(1)} collective-permute-done((f32[8,128]{1,0:T(8,128)S(1)}, f32[8,128]{1,0:T(8,128)S(1)}, u32[]{:S(2)}, u32[]{:S(2)}) %collective-permute-start.2) | collective-permute-done | bytes 4128 | tf_op jit(solution)/shard_map/ppermute | solution.py:455
  10.6 0.0 collective-permute-done
  10.6 0.0 collective-permute-done.1
  10.7 1.6 %collective-permute-start.5 = (f32[56,128]{1,0:T(8,128)S(1)}, f32[56,128]{1,0:T(8,128)S(1)}, u32[]{:S(2)}, u32[]{:S(2)}) collective-permute-start(f32[56,128]{1,0:T(8,128)S(1)} %get-tuple-element.52), channel_id=1, source_target_pairs={{0,4},{4,0},{8,12},{12,8},{16,20},{20,16},{24,28},{28,24},{1,5},{5... | collective-permute-start | bytes 86024 | tf_op jit(solution)/shard_map/ppermute | solution.py:455
  12.2 1.6 %collective-permute-start.4 = (f32[56,128]{1,0:T(8,128)S(1)}, f32[56,128]{1,0:T(8,128)S(1)}, u32[]{:S(2)}, u32[]{:S(2)}) collective-permute-start(f32[56,128]{1,0:T(8,128)S(1)} %get-tuple-element.51), channel_id=1, source_target_pairs={{0,8},{4,12},{8,0},{12,4},{16,24},{20,28},{24,16},{28,20},{1,9},{5... | collective-permute-start | bytes 86024 | tf_op jit(solution)/shard_map/ppermute | solution.py:455
  13.8 0.4 %collective-permute-start.3 = (f32[64,128]{1,0:T(8,128)S(1)}, f32[64,128]{1,0:T(8,128)S(1)}, u32[]{:S(2)}, u32[]{:S(2)}) collective-permute-start(f32[64,128]{1,0:T(8,128)S(1)} %pad_maximum_fusion.2), channel_id=1, source_target_pairs={{0,12},{4,8},{8,4},{12,0},{16,28},{20,24},{24,20},{28,16},{1,13},{... | collective-permute-start | bytes 98312 | tf_op jit(solution)/shard_map/ppermute | solution.py:455
  14.2 0.4 %collective-permute-done.5 = f32[56,128]{1,0:T(8,128)S(1)} collective-permute-done((f32[56,128]{1,0:T(8,128)S(1)}, f32[56,128]{1,0:T(8,128)S(1)}, u32[]{:S(2)}, u32[]{:S(2)}) %collective-permute-start.5) | collective-permute-done | bytes 28704 | tf_op jit(solution)/shard_map/ppermute | solution.py:455
  14.6 1.5 %collective-permute-done.4 = f32[56,128]{1,0:T(8,128)S(1)} collective-permute-done((f32[56,128]{1,0:T(8,128)S(1)}, f32[56,128]{1,0:T(8,128)S(1)}, u32[]{:S(2)}, u32[]{:S(2)}) %collective-permute-start.4) | collective-permute-done | bytes 28704 | tf_op jit(solution)/shard_map/ppermute | solution.py:455
  16.1 2.5 %collective-permute-done.3 = f32[64,128]{1,0:T(8,128)S(1)} collective-permute-done((f32[64,128]{1,0:T(8,128)S(1)}, f32[64,128]{1,0:T(8,128)S(1)}, u32[]{:S(2)}, u32[]{:S(2)}) %collective-permute-start.3) | collective-permute-done | bytes 32800 | tf_op jit(solution)/shard_map/ppermute | solution.py:455
  18.7 0.5 %shard_map.94 = (f32[6,16,128]{2,1,0:T(8,128)S(1)}, f32[8,128]{1,0:T(8,128)S(1)}) custom-call(f32[48,128]{1,0:T(8,128)S(1)} %get-tuple-element.35.ring_a, f32[48,128]{1,0:T(8,128)S(1)} %get-tuple-element.34.ring_b, f32[8,8,128]{2,1,0:T(8,128)S(1)} %bitcast.52, f32[6,16,128]{2,1,0:T(8,128)S(1)} %get-tuple-element.18.flow, ...), custom_call_target="tpu_custom_call" | custom-call | tf_op jit(solution)/shard_map/pallas_call | solution.py:585
  19.1 2.0 %collective-permute-start.6 = (f32[40,128]{1,0:T(8,128)S(1)}, f32[40,128]{1,0:T(8,128)S(1)}, u32[]{:S(2)}, u32[]{:S(2)}) collective-permute-start(f32[40,128]{1,0:T(8,128)S(1)} %pad_maximum_fusion.4), channel_id=1, source_target_pairs={{0,16},{4,20},{8,24},{12,28},{16,0},{20,4},{24,8},{28,12},{1,17},{... | collective-permute-start | bytes 61448 | tf_op jit(solution)/shard_map/ppermute | solution.py:455
  21.2 0.6 %shard_map.96.sweep = f32[6,16,128]{2,1,0:T(8,128)S(1)} custom-call(f32[6,16,128]{2,1,0:T(8,128)S(1)} %get-tuple-element.30.residual, f32[36,16,128]{2,1,0:T(8,128)S(1)} %get-tuple-element.25.gain, f32[6,16,128]{2,1,0:T(8,128)S(1)} %get-tuple-element.26.source, f32[288,16,128]{2,1,0:T(8,128)S(1)} %get-tuple-element.24.scan), custom_call_target="tpu_custom_call" | custom-call | flops 1048576 | bytes 2097152 | tf_op jit(solution)/shard_map/pallas_call | solution.py:591
  21.8 2.2 %collective-permute-done.6 = f32[40,128]{1,0:T(8,128)S(1)} collective-permute-done((f32[40,128]{1,0:T(8,128)S(1)}, f32[40,128]{1,0:T(8,128)S(1)}, u32[]{:S(2)}, u32[]{:S(2)}) %collective-permute-start.6) | collective-permute-done | bytes 20512 | tf_op jit(solution)/shard_map/ppermute | solution.py:455
  23.9 0.5 %collective-permute-start.7 = (f32[8,128]{1,0:T(8,128)S(1)}, f32[8,128]{1,0:T(8,128)S(1)}, u32[]{:S(2)}, u32[]{:S(2)}) collective-permute-start(f32[8,128]{1,0:T(8,128)S(1)} %slice_add_fusion), channel_id=1, source_target_pairs={{0,4},{4,0},{8,12},{12,8},{16,20},{20,16},{24,28},{28,24},{1,5},{5... | collective-permute-start | bytes 12296 | tf_op jit(solution)/shard_map/ppermute | solution.py:455
  24.4 0.3 %collective-permute-start.8 = (f32[8,128]{1,0:T(8,128)S(1)}, f32[8,128]{1,0:T(8,128)S(1)}, u32[]{:S(2)}, u32[]{:S(2)}) collective-permute-start(f32[8,128]{1,0:T(8,128)S(1)} %slice_add_fusion), channel_id=1, source_target_pairs={{0,8},{4,12},{8,0},{12,4},{16,24},{20,28},{24,16},{28,20},{1,9},{5... | collective-permute-start | bytes 12296 | tf_op jit(solution)/shard_map/ppermute | solution.py:455
  24.8 2.6 %collective-permute-start.9 = (f32[8,128]{1,0:T(8,128)S(1)}, f32[8,128]{1,0:T(8,128)S(1)}, u32[]{:S(2)}, u32[]{:S(2)}) collective-permute-start(f32[8,128]{1,0:T(8,128)S(1)} %slice_add_fusion), channel_id=1, source_target_pairs={{0,12},{4,8},{8,4},{12,0},{16,28},{20,24},{24,20},{28,16},{1,13},{... | collective-permute-start | bytes 12296 | tf_op jit(solution)/shard_map/ppermute | solution.py:455
  27.4 0.9 %shard_map.95.weights = f32[48,128]{1,0:T(8,128)S(1)} custom-call(f32[8,8,128]{2,1,0:T(8,128)S(1)} %pad_maximum_fusion.3.ring), custom_call_target="tpu_custom_call" | custom-call | tf_op jit(solution)/shard_map/pallas_call | solution.py:601
  28.4 0.0 collective-permute-done.7
  28.4 0.0 collective-permute-done.8
  28.4 0.9 %collective-permute-done.9 = f32[8,128]{1,0:T(8,128)S(1)} collective-permute-done((f32[8,128]{1,0:T(8,128)S(1)}, f32[8,128]{1,0:T(8,128)S(1)}, u32[]{:S(2)}, u32[]{:S(2)}) %collective-permute-start.9) | collective-permute-done | bytes 4128 | tf_op jit(solution)/shard_map/ppermute | solution.py:455
  29.3 0.7 %shard_map.97 = f32[6,16,128]{2,1,0:T(8,128)} custom-call(f32[8,128]{1,0:T(8,128)S(1)} %add_add_fusion.gathered, f32[48,128]{1,0:T(8,128)S(1)} %shard_map.95.weights, f32[6,16,128]{2,1,0:T(8,128)S(1)} %get-tuple-element.18.flow, f32[288,16,128]{2,1,0:T(8,128)S(1)} %get-tuple-element.24.scan, f32[6,16,128]{2,1,0:T(8,128)S(1)} %shard_map.96.sweep), custom_call_target="tpu_custom_call" | custom-call | tf_op jit(solution)/shard_map/pallas_call | solution.py:610
  (21 shorter events, 0.1 us)
Async XLA Ops:
  0.9 9.7 %collective-permute-start = (f32[48,128]{1,0:T(8,128)S(1)}, f32[48,128]{1,0:T(8,128)S(1)}, u32[]{:S(2)}, u32[]{:S(2)}) collective-permute-start(f32[48,128]{1,0:T(8,128)S(1)} %get-tuple-element.21), channel_id=1, source_target_pairs={{0,17},{1,18},{2,19},{3,16},{4,21},{5,22},{6,23},{7,20},{8,25},{9,... | collective-permute-start | bytes 73736 | tf_op jit(solution)/shard_map/ppermute | solution.py:459
  4.5 6.1 %collective-permute-start.1 = (f32[48,128]{1,0:T(8,128)S(1)}, f32[48,128]{1,0:T(8,128)S(1)}, u32[]{:S(2)}, u32[]{:S(2)}) collective-permute-start(f32[48,128]{1,0:T(8,128)S(1)} %get-tuple-element.21), channel_id=1, source_target_pairs={{0,1},{1,2},{2,3},{3,0},{4,5},{5,6},{6,7},{7,4},{8,9},{9,10},{10,1... | collective-permute-start | bytes 73736 | tf_op jit(solution)/shard_map/ppermute | solution.py:459
  6.1 4.5 %collective-permute-start.2 = (f32[8,128]{1,0:T(8,128)S(1)}, f32[8,128]{1,0:T(8,128)S(1)}, u32[]{:S(2)}, u32[]{:S(2)}) collective-permute-start(f32[8,128]{1,0:T(8,128)S(1)} %get-tuple-element.19.halo), channel_id=1, source_target_pairs={{0,16},{4,20},{8,24},{12,28},{16,0},{20,4},{24,8},{28,12},{1,17},{... | collective-permute-start | bytes 12296 | tf_op jit(solution)/shard_map/ppermute | solution.py:455
  10.7 3.9 %collective-permute-start.5 = (f32[56,128]{1,0:T(8,128)S(1)}, f32[56,128]{1,0:T(8,128)S(1)}, u32[]{:S(2)}, u32[]{:S(2)}) collective-permute-start(f32[56,128]{1,0:T(8,128)S(1)} %get-tuple-element.52), channel_id=1, source_target_pairs={{0,4},{4,0},{8,12},{12,8},{16,20},{20,16},{24,28},{28,24},{1,5},{5... | collective-permute-start | bytes 86024 | tf_op jit(solution)/shard_map/ppermute | solution.py:455
  12.2 3.9 %collective-permute-start.4 = (f32[56,128]{1,0:T(8,128)S(1)}, f32[56,128]{1,0:T(8,128)S(1)}, u32[]{:S(2)}, u32[]{:S(2)}) collective-permute-start(f32[56,128]{1,0:T(8,128)S(1)} %get-tuple-element.51), channel_id=1, source_target_pairs={{0,8},{4,12},{8,0},{12,4},{16,24},{20,28},{24,16},{28,20},{1,9},{5... | collective-permute-start | bytes 86024 | tf_op jit(solution)/shard_map/ppermute | solution.py:455
  13.8 4.8 %collective-permute-start.3 = (f32[64,128]{1,0:T(8,128)S(1)}, f32[64,128]{1,0:T(8,128)S(1)}, u32[]{:S(2)}, u32[]{:S(2)}) collective-permute-start(f32[64,128]{1,0:T(8,128)S(1)} %pad_maximum_fusion.2), channel_id=1, source_target_pairs={{0,12},{4,8},{8,4},{12,0},{16,28},{20,24},{24,20},{28,16},{1,13},{... | collective-permute-start | bytes 98312 | tf_op jit(solution)/shard_map/ppermute | solution.py:455
  19.1 4.8 %collective-permute-start.6 = (f32[40,128]{1,0:T(8,128)S(1)}, f32[40,128]{1,0:T(8,128)S(1)}, u32[]{:S(2)}, u32[]{:S(2)}) collective-permute-start(f32[40,128]{1,0:T(8,128)S(1)} %pad_maximum_fusion.4), channel_id=1, source_target_pairs={{0,16},{4,20},{8,24},{12,28},{16,0},{20,4},{24,8},{28,12},{1,17},{... | collective-permute-start | bytes 61448 | tf_op jit(solution)/shard_map/ppermute | solution.py:455
  23.9 4.4 %collective-permute-start.7 = (f32[8,128]{1,0:T(8,128)S(1)}, f32[8,128]{1,0:T(8,128)S(1)}, u32[]{:S(2)}, u32[]{:S(2)}) collective-permute-start(f32[8,128]{1,0:T(8,128)S(1)} %slice_add_fusion), channel_id=1, source_target_pairs={{0,4},{4,0},{8,12},{12,8},{16,20},{20,16},{24,28},{28,24},{1,5},{5... | collective-permute-start | bytes 12296 | tf_op jit(solution)/shard_map/ppermute | solution.py:455
  24.4 3.9 %collective-permute-start.8 = (f32[8,128]{1,0:T(8,128)S(1)}, f32[8,128]{1,0:T(8,128)S(1)}, u32[]{:S(2)}, u32[]{:S(2)}) collective-permute-start(f32[8,128]{1,0:T(8,128)S(1)} %slice_add_fusion), channel_id=1, source_target_pairs={{0,8},{4,12},{8,0},{12,4},{16,24},{20,28},{24,16},{28,20},{1,9},{5... | collective-permute-start | bytes 12296 | tf_op jit(solution)/shard_map/ppermute | solution.py:455
  24.8 4.5 %collective-permute-start.9 = (f32[8,128]{1,0:T(8,128)S(1)}, f32[8,128]{1,0:T(8,128)S(1)}, u32[]{:S(2)}, u32[]{:S(2)}) collective-permute-start(f32[8,128]{1,0:T(8,128)S(1)} %slice_add_fusion), channel_id=1, source_target_pairs={{0,12},{4,8},{8,4},{12,0},{16,28},{20,24},{24,20},{28,16},{1,13},{... | collective-permute-start | bytes 12296 | tf_op jit(solution)/shard_map/ppermute | solution.py:455
